TPU v7x, 512 devices: a whole 4x4x16 slice. The times are simulated.
512 devices in a mesh: sub: 16 (over z), row: 4 (over y), col: 8 (over x, core).
Axes of the slice: x: 4, y: 4, z: 16, core: 2. Of those that a mesh axis runs over, the one named last changes fastest.
Arguments:
- child_factor: float32 [16, 256, 2048], P('sub', None, 'row'), may hold values from -6 to 6
- child_map: int32 [16, 2048], P('sub'), may hold values from 0 to 8191, as said below
- child_len: int32 [16], P('sub'), may hold values from 1 to 2048, 16384 in all
- class_ids: int32 [8192], replicated, may hold values from 0 to 7
- class_kappa: float32 [8], replicated, may hold values from 0.25 to 16
- landmarks: int32 [256], replicated, may hold values from 0 to 1023
- diag_inverse: float32 [2, 512, 512], replicated, as said below
Outputs:
- panel_factor: float32 [2, 512, 16, 512], P(None, 'col', 'sub', 'row')
- landmark_solution: float32 [256, 16, 512], P('col', 'sub', 'row')
Inputs may be any that keep to these rules, and one draw needn't show every extreme that they name: `child_map`: node i of a child maps to parent row 512 a + 128 (i // 512) + u for some block a and some u below 128; the nodes of one child map to distinct rows. `diag_inverse`: each 512 x 512 block is lower triangular with a positive diagonal.
All inputs are finite; a program needn't handle non-finite values. No bound on the sum of `child_len` on one device may be relied on, other than what follows from the above.
Results may differ from a plain program's by a relative error of at most 0.0003.
Values sent between devices are 32-bit elements; how exact they have to be, the bound alone decides.
A program may use at most 64 MiB of HBM per device.

v0:
```python
import jax
import jax.numpy as jnp
from jax import lax
from jax.sharding import PartitionSpec as P

PRECISE = lax.Precision.HIGHEST


def from_root(value, axis, root):
    mine = lax.axis_index(axis) == root
    return lax.psum(jnp.where(mine, value, jnp.zeros_like(value)), axis)


def contract(left_part, right_part, left_dim, right_dim):
    return lax.dot_general(
        left_part,
        right_part,
        (((left_dim,), (right_dim,)), ((), ())),
        precision=PRECISE,
        preferred_element_type=jnp.float32,
    )


def on_device(child_factor, child_map, child_len, class_ids, class_kappa, landmarks, diag_inverse):
    sub_index = lax.axis_index("sub")
    row_index = lax.axis_index("row")
    col_index = lax.axis_index("col")
    sub_count = lax.axis_size("sub")
    row_count = lax.axis_size("row")
    col_count = lax.axis_size("col")
    panels = diag_inverse.shape[0]
    width_panel = diag_inverse.shape[1]
    total_nodes = class_ids.shape[0]
    col_width = width_panel // col_count
    quarter = width_panel // row_count
    quarter_rows = total_nodes // row_count
    local_rows = quarter_rows // sub_count
    blocks_local = local_rows // quarter
    node_quarter = child_factor.shape[2]
    own_cols = (
        jnp.arange(panels, dtype=jnp.int32)[:, None] * width_panel
        + col_index * col_width
        + jnp.arange(col_width, dtype=jnp.int32)[None, :]
    ).reshape(-1)
    node_map = child_map[0]
    node_index = row_index * node_quarter + jnp.arange(node_quarter, dtype=jnp.int32)
    live_factor = jnp.where((node_index < child_len[0])[None, :], child_factor[0], jnp.float32(0.0))
    select = (node_map[:, None] == own_cols[None, :]).astype(jnp.float32)
    reduced = jnp.dot(
        lax.all_gather(live_factor, "row", axis=1, tiled=True), select, precision=PRECISE
    )
    partial_cols = jnp.zeros((node_quarter, own_cols.shape[0]), jnp.float32) - contract(
        live_factor, reduced, 0, 0
    )
    parent = lax.dynamic_slice_in_dim(node_map, row_index * node_quarter, node_quarter)
    target = parent // width_panel * quarter + parent % width_panel - row_index * quarter
    place_rows = (target[:, None] == jnp.arange(quarter_rows, dtype=jnp.int32)[None, :]).astype(
        jnp.float32
    )
    contribution = contract(partial_cols, place_rows, 0, 0)
    front_cols = lax.psum_scatter(contribution, "sub", scatter_dimension=1, tiled=True)
    class_table = (
        class_ids[:, None] == jnp.arange(class_kappa.shape[0], dtype=jnp.int32)[None, :]
    ).astype(jnp.float32)
    coefficient = jnp.sum(class_table * class_kappa[None, :], axis=1) + jnp.float32(4.0)
    local_index = jnp.arange(local_rows, dtype=jnp.int32)
    global_rows = (
        (sub_index * blocks_local + local_index // quarter) * width_panel
        + row_index * quarter
        + local_index % quarter
    )
    coeff_row = jnp.take(coefficient, global_rows)[None, :]
    coeff_col = jnp.take(coefficient, own_cols)[:, None]
    offset_band = global_rows[None, :] - own_cols[:, None]
    end_count = jnp.where(
        (global_rows == 0) | (global_rows == total_nodes - 1), jnp.float32(1.0), jnp.float32(2.0)
    )[None, :]
    band_part = jnp.where(
        offset_band == 0,
        coeff_row * coeff_row + end_count,
        jnp.where(
            jnp.abs(offset_band) == 1,
            -(coeff_row + coeff_col),
            jnp.where(jnp.abs(offset_band) == 2, jnp.float32(1.0), jnp.float32(0.0)),
        ),
    )
    front_cols = front_cols + band_part
    land_count = landmarks.shape[0] // col_count
    chooser = (landmarks[:, None] == own_cols[None, :]).astype(jnp.float32)
    right_side = lax.psum_scatter(
        jnp.dot(chooser, front_cols, precision=PRECISE), "col", scatter_dimension=0, tiled=True
    )
    column_slabs = [slab for slab in front_cols.reshape(panels, col_width, local_rows)]
    inner_index = jnp.arange(width_panel, dtype=jnp.int32)
    block_of_row = global_rows // width_panel
    pieces = []
    for panel_index in range(panels):
        inverse = diag_inverse[panel_index]
        panel_now = contract(
            lax.all_gather(column_slabs[panel_index], "col", axis=0, tiled=True), inverse, 0, 1
        )
        keep_mask = global_rows[:, None] - panel_index * width_panel >= inner_index[None, :]
        panel_now = jnp.where(keep_mask, panel_now, jnp.float32(0.0))
        pieces.append(lax.dynamic_slice_in_dim(panel_now, col_index * col_width, col_width, 1).T)
        for later_panel in range(panel_index + 1, panels):
            owner_sub = later_panel // blocks_local
            whole_block = from_root(
                lax.all_gather(panel_now, "row", axis=0, tiled=True), "sub", owner_sub
            )
            my_slice = lax.dynamic_slice_in_dim(whole_block, col_index * col_width, col_width, 0)
            column_slabs[later_panel] = column_slabs[later_panel] - contract(
                my_slice, panel_now, 1, 1
            )
        owner_sub = panel_index // blocks_local
        gathered = lax.all_gather(right_side, "row", axis=1, tiled=True)
        values = from_root(contract(gathered, inverse, 1, 1), "sub", owner_sub)
        below_update = contract(values, panel_now, 1, 1)
        settled = jnp.tile(
            lax.dynamic_slice_in_dim(values, row_index * quarter, quarter, 1), (1, blocks_local)
        )
        right_side = jnp.where(
            (block_of_row > panel_index)[None, :],
            right_side - below_update,
            jnp.where((block_of_row == panel_index)[None, :], settled, right_side),
        )
    panel_factor = jnp.stack(pieces).reshape(panels, col_width, blocks_local, quarter)
    landmark_solution = right_side.reshape(land_count, blocks_local, quarter)
    return (panel_factor, landmark_solution)


def solution(mesh):
    return jax.shard_map(
        on_device,
        mesh=mesh,
        in_specs=(P("sub", None, "row"), P("sub", None), P("sub"), P(), P(), P(), P()),
        out_specs=(P(None, "col", "sub", "row"), P("col", "sub", "row")),
        check_vma=False,
    )
```

profile of v0, /device:TPU:1, one launch (start us, length us, event | category | flops | bytes accessed | tf_op | source)
XLA Modules:
  0.0 513.7 jit_solution(16760685932046861145)
XLA Ops:
  7.2 0.0 all-gather.3.cloned.1.call-start
  7.9 1.9 bitcast_select_fusion
  9.8 0.0 copy-start.2
  9.8 0.0 all-gather.3.cloned.1.call-update
  9.8 0.0 reduce-scatter.3.cloned.1.call-start
  9.9 0.1 iota_add_fusion
  9.9 0.1 add.292
  10.0 0.7 constant_dynamic-slice_fusion
  10.7 43.3 %all-gather.3.cloned.1.call-done = f32[256,2048]{1,0:T(8,128)} async-done(((f32[256,512]{1,0:T(8,128)}), f32[256,2048]{1,0:T(8,128)}) %all-gather.3.cloned.1.call-update) | async-done | bytes 2097168 | tf_op jit(solution)/shard_map/all_gather | solution.py:50
  54.0 2.8 fusion.8
  56.8 0.0 copy-done.2
  56.8 0.0 copy-start.5
  56.8 0.0 copy-start.7
  56.8 1.0 convolution_subtract_fusion
  57.8 0.0 copy-start.6
  57.9 0.0 copy-start
  57.9 2.7 fusion
  60.5 0.0 reduce-scatter.3.cloned.1.call-update
  60.5 0.0 reduce-scatter.5.cloned.1.call-start
  60.6 0.0 copy-done.5
  60.7 0.0 copy-done.7
  60.7 0.1 select_reduce_fusion
  60.8 1.1 gather_fusion
  62.0 1.1 gather_fusion.1
  63.2 58.0 %reduce-scatter.3.cloned.1.call-done = f32[128,128]{1,0:T(8,128)} async-done(((f32[128,2048]{1,0:T(8,128)}), f32[128,128]{1,0:T(8,128)}) %reduce-scatter.3.cloned.1.call-update) | async-done | bytes 65552 | tf_op jit(solution)/shard_map/reduce_scatter | solution.py:61
  121.2 0.9 select_add_fusion
  122.2 0.0 copy-done.6
  122.2 0.9 fusion.17
  123.1 0.0 reduce-scatter.5.cloned.1.call-update
  123.1 0.0 all-reduce.4.cloned.1.call-start
  123.2 23.6 %all_gather.19 = f32[512,128]{1,0:T(8,128)S(1)} all-gather(f32[64,128]{1,0:T(8,128)S(1)} %unstack.10), channel_id=1, replica_groups=mesh['sub'=16,'row'=4,'col'=8] {'col'}, dimensions={0}, use_global_device_ids=true | all-gather | bytes 294912 | tf_op jit(solution)/shard_map/all_gather | solution.py:100
  146.8 21.6 %reduce-scatter.5.cloned.1.call-done = f32[32,128]{1,0:T(8,128)} async-done(((f32[256,128]{1,0:T(8,128)}), f32[32,128]{1,0:T(8,128)}) %reduce-scatter.5.cloned.1.call-update) | async-done | bytes 16400 | tf_op jit(solution)/shard_map/reduce_scatter | solution.py:90
  168.4 0.0 copy-start.3
  168.4 9.3 %all_gather.22 = f32[32,512]{1,0:T(8,128)S(1)} all-gather(f32[32,128]{1,0:T(8,128)} %reduce-scatter.5.cloned.1.call-done), channel_id=1, replica_groups=mesh['sub'=16,'row'=4,'col'=8] {'row'}, dimensions={1}, use_global_device_ids=true | all-gather | bytes 81920 | tf_op jit(solution)/shard_map/all_gather | solution.py:115
  177.7 0.0 copy-done
  177.7 1.7 convolution_select_fusion.3
  179.3 0.0 all-reduce.4.cloned.1.call-update
  179.4 0.0 all-gather.5.cloned.1.call-start
  179.4 2.0 convolution_select_fusion.1
  181.4 0.0 all-gather.5.cloned.1.call-update
  181.4 0.0 all-reduce.6.cloned.1.call-start
  181.5 123.4 %all-reduce.4.cloned.1.call-done = f32[32,512]{1,0:T(8,128)} async-done(((f32[32,512]{1,0:T(8,128)}), f32[32,512]{1,0:T(8,128)}) %all-reduce.4.cloned.1.call-update) | async-done | bytes 65552 | tf_op jit(solution)/shard_map/psum | solution.py:11
  304.9 0.0 copy-done.3
  304.9 1.3 fusion.3
  306.2 9.7 %all_gather.23 = f32[32,512]{1,0:T(8,128)S(1)} all-gather(f32[32,128]{1,0:T(8,128)S(1)} %fusion.3), channel_id=1, replica_groups=mesh['sub'=16,'row'=4,'col'=8] {'row'}, dimensions={1}, use_global_device_ids=true | all-gather | bytes 81920 | tf_op jit(solution)/shard_map/all_gather | solution.py:115
  316.0 0.0 copy-start.1
  316.0 1.7 convolution_select_fusion.2
  317.7 27.0 %all-gather.5.cloned.1.call-done = f32[512,512]{1,0:T(8,128)} async-done(((f32[128,512]{1,0:T(8,128)}), f32[512,512]{1,0:T(8,128)}) %all-gather.5.cloned.1.call-update) | async-done | bytes 1048592 | tf_op jit(solution)/shard_map/all_gather | solution.py:108
  344.7 1.1 broadcast_select_fusion
  345.8 0.0 all-reduce.6.cloned.1.call-update
  345.8 0.0 copy-done.1
  345.8 0.1 dynamic-slice_bitcast_fusion.1
  345.9 133.4 %all-reduce.6.cloned.1.call-done = (f32[512,512]{1,0:T(8,128)}, f32[32,512]{1,0:T(8,128)}) async-done(((f32[512,512]{1,0:T(8,128)}, f32[32,512]{1,0:T(8,128)}), (f32[512,512]{1,0:T(8,128)}, f32[32,512]{1,0:T(8,128)})) %all-reduce.6.cloned.1.call-update) | async-done | bytes 1114128 | tf_op jit(solution)/shard_map/psum | solution.py:11
  479.3 0.0 copy-start.4
  479.3 1.3 convolution_subtract_fusion.1
  480.6 23.2 %all_gather.21 = f32[512,128]{1,0:T(8,128)S(1)} all-gather(f32[64,128]{1,0:T(8,128)S(1)} %convolution_subtract_fusion.1), channel_id=1, replica_groups=mesh['sub'=16,'row'=4,'col'=8] {'col'}, dimensions={0}, use_global_device_ids=true | all-gather | bytes 294912 | tf_op jit(solution)/shard_map/all_gather | solution.py:100
  503.8 1.3 convolution_select_fusion
  505.1 0.1 dynamic-slice_bitcast_fusion
  505.2 0.7 copy.13
  505.9 0.0 copy-done.4
  505.9 1.0 fusion.2
  (13 shorter events, 0.1 us)
Async XLA Ops:
  7.2 46.8 %all-gather.3.cloned.1.call-start = ((), (), s32[]{:S(2)}) async-start(), calls=%async_computation.2 | async-start | bytes 2621440 | tf_op jit(solution)/shard_map/all_gather | solution.py:50
  9.8 47.0 %copy-start.2 = (f32[256,512]{1,0:T(8,128)S(1)}, f32[256,512]{1,0:T(8,128)}, u32[]{:S(2)}) copy-start(f32[256,512]{1,0:T(8,128)} %bitcast_select_fusion) | copy-start | bytes 1572868
  9.8 111.4 %reduce-scatter.3.cloned.1.call-start = ((), (), s32[]{:S(2)}) async-start(), calls=%async_computation.3 | async-start | bytes 1114112 | tf_op jit(solution)/shard_map/reduce_scatter | solution.py:61
  56.8 3.8 copy-start.5
  56.8 3.8 copy-start.7
  57.8 64.3 %copy-start.6 = (s32[256]{0:T(256)S(1)}, s32[256]{0:T(256)}, u32[]{:S(2)}) copy-start(s32[256]{0:T(256)} %param.14) | copy-start | bytes 3076
  57.9 119.8 %copy-start = (f32[2,512,512]{2,1,0:T(8,128)S(1)}, f32[2,512,512]{2,1,0:T(8,128)}, u32[]{:S(2)}) copy-start(f32[2,512,512]{2,1,0:T(8,128)} %param.15) | copy-start | bytes 6291460
  60.5 107.8 %reduce-scatter.5.cloned.1.call-start = ((), (), s32[]{:S(2)}) async-start(), calls=%async_computation.5 | async-start | bytes 147456 | tf_op jit(solution)/shard_map/reduce_scatter | solution.py:90
  123.1 181.8 %all-reduce.4.cloned.1.call-start = ((), (), s32[]{:S(2)}) async-start(), calls=%async_computation.6 | async-start | bytes 131072 | tf_op jit(solution)/shard_map/psum | solution.py:11
  168.4 136.6 %copy-start.3 = (f32[32,128]{1,0:T(8,128)S(1)}, f32[32,128]{1,0:T(8,128)}, u32[]{:S(2)}) copy-start(f32[32,128]{1,0:T(8,128)} %reduce-scatter.5.cloned.1.call-done) | copy-start | bytes 49156
  179.4 165.3 %all-gather.5.cloned.1.call-start = ((), (), s32[]{:S(2)}) async-start(), calls=%async_computation.4 | async-start | bytes 1310720 | tf_op jit(solution)/shard_map/all_gather | solution.py:108
  181.4 297.9 %all-reduce.6.cloned.1.call-start = ((), (), s32[]{:S(2)}) async-start(), calls=%async_computation.7 | async-start | bytes 2228224 | tf_op jit(solution)/shard_map/psum | solution.py:11
  316.0 29.8 %copy-start.1 = (f32[128,512]{1,0:T(8,128)S(1)}, f32[128,512]{1,0:T(8,128)}, u32[]{:S(2)}) copy-start(f32[128,512]{1,0:T(8,128)} %convolution_select_fusion.1) | copy-start | bytes 786436
  479.3 26.6 %copy-start.4 = (f32[32,512]{1,0:T(8,128)S(1)}, f32[32,512]{1,0:T(8,128)}, u32[]{:S(2)}) copy-start(f32[32,512]{1,0:T(8,128)} %get-tuple-element.10) | copy-start | bytes 196612
Sparse Core Ops, SparseCore 0:
  10.1 43.8 all-gather.2
  60.7 60.4 reduce-scatter.2
  124.2 44.0 reduce-scatter.4
  179.5 125.3 all-reduce.3
  307.1 37.5 all-gather.4
  347.7 131.5 all-reduce.5
where the time goes:
time: 514 us
  waiting for transfers between devices  407 us (79%)
  blocking collectives  65.8 us (13%)
  matrix products  17.6 us (3%)
  between operations  15 us (3%)
    psum x2, waiting for transfers between devices, from_root(): return lax.psum(jnp.where(mine, value, jnp.zeros_like(value)), axis)  257 us
    reduce_scatter x1, waiting for transfers between devices, on_device(): lax.psum_scatter(contribution, 'sub', scatter_dimension=1, tiled=True)  58 us
    all_gather x2, blocking collectives, on_device(): lax.all_gather(column_slabs[panel_index], 'col', axis=0, tiled=True)  46.8 us
    all_gather x1, waiting for transfers between devices, on_device(): lax.all_gather(live_factor, 'row', axis=1, tiled=True)  43.3 us
    all_gather x1, waiting for transfers between devices, on_device(): lax.all_gather(panel_now, 'row', axis=0, tiled=True)  27 us
    reduce_scatter x1, waiting for transfers between devices, on_device(): lax.psum_scatter(jnp.dot(chooser, front_cols, precision=PRECISE), 'col',...  21.6 us
    all_gather x2, blocking collectives, on_device(): gathered = lax.all_gather(right_side, 'row', axis=1, tiled=True)  19 us
    dot_general x9, matrix products, contract(): lax.dot_general(left_part, right_part, (((left_dim,), (right_dim,)), ((),...  13.9 us
  transfers between devices with their start and end apart: 6, of which 6 were waited for; matrix products, arithmetic and copies ran while one was open for 2% of the time, Pallas kernels for 0%

commit v1 on v0

v1 whole, which is shorter than its diff:
```python
import jax
import jax.numpy as jnp
from jax import lax
from jax.experimental import pallas as pl
from jax.experimental.pallas import tpu as pltpu
from jax.sharding import PartitionSpec as P

F32 = jnp.float32
BF16 = jnp.bfloat16
MESH = pl.DeviceIdType.MESH

NSUB, NROW, NCOL = 16, 4, 8
PW, Q, CW, KCH, NODEQ, NLAND = 512, 128, 64, 256, 512, 32
CHUNKS = 2
CROWS = 2 * CW // CHUNKS


def dg(a, b, ca, cb):
    return lax.dot_general(a, b, (((ca,), (cb,)), ((), ())), preferred_element_type=F32)


def split(x):
    hi = x.astype(BF16)
    return hi, (x - hi.astype(F32)).astype(BF16)


def mm(a, b_hi, b_lo, cb):
    n = a.shape[0]
    a_hi, a_lo = split(a)
    both = dg(jnp.concatenate([a_hi, a_lo], axis=0), b_hi, 1, cb)
    return both[:n] + both[n:] + dg(a_hi, b_lo, 1, cb)


def lanes(shape):
    return lax.broadcasted_iota(jnp.int32, shape, 1)


def rows_of(shape):
    return lax.broadcasted_iota(jnp.int32, shape, 0)


def kernel(
    factor_hbm, map_ref, len_ref, ids_ref, kappa_ref, land_ref, dinv_hbm,
    pf_ref, ls_ref,
    factor, dinv, live_hi, live_lo, red_out, red_in, redl, pst,
    top_out, top_in, top_own, top_all, front_top, rland, s_hi, s_lo,
    first, ring_p, ring_m, fx,
    ld_sem, red_s, red_r, redl_s, redl_r, top_s, top_r, tag_s, tag_r,
    pla_s, pla_r, fwd_s, fwd_r, rl_s, rl_r,
    rp_s, rp_r, rm_s, rm_r, xa_s, xa_r, xf_s, xf_r,
):
    s = lax.axis_index("sub")
    r = lax.axis_index("row")
    c = lax.axis_index("col")
    x, h = c // 2, c % 2
    other = {"col": 2 * x + 1 - h}
    group = 2 * ((r + x) % NROW) + h

    load_factor = pltpu.make_async_copy(factor_hbm.at[0], factor, ld_sem.at[0])
    load_factor.start()
    load_dinv = pltpu.make_async_copy(dinv_hbm, dinv, ld_sem.at[1])
    load_dinv.start()
    barrier = pltpu.get_barrier_semaphore()

    def greet_z(k, carry):
        pl.semaphore_signal(barrier, inc=1, device_id={"sub": (s + k) % NSUB}, device_id_type=MESH)
        return carry

    def plane_peer(k):
        m = (r * 4 + x + k) % 16
        return m // 4, m % 4

    def greet_plane(k, carry):
        pr, px = plane_peer(k)
        pl.semaphore_signal(barrier, inc=1, device_id={"row": pr, "col": 2 * px + h}, device_id_type=MESH)
        return carry

    lax.fori_loop(1, NSUB, greet_z, 0)
    lax.fori_loop(1, 16, greet_plane, 0)
    pl.semaphore_signal(barrier, inc=1, device_id=other, device_id_type=MESH)

    node_row = map_ref[:, pl.ds(pl.multiple_of(r * NODEQ, NODEQ), NODEQ)]
    land_row = land_ref[...]
    land_col = jnp.sum(
        jnp.where(lanes((NLAND, 256)) == rows_of((NLAND, 256)) + c * NLAND, land_row.astype(F32), 0.0),
        axis=1, keepdims=True,
    ).astype(jnp.int32)
    iota_col = rows_of((2 * CW, 1))
    send_cols = iota_col // CW * PW + (2 * r + h) * CW + iota_col % CW
    own_cols = iota_col // CW * PW + group * CW + iota_col % CW
    select = jnp.concatenate([send_cols, land_col], axis=0) == node_row
    select = jnp.where(select, 1.0, 0.0).astype(BF16)
    load_factor.wait()
    live = jnp.where(lanes((KCH, NODEQ)) + r * NODEQ < len_ref[0], factor[...], 0.0)
    lh, ll = split(live)
    live_hi[...] = lh
    live_lo[...] = ll
    reduced = dg(select, lh, 1, 1) + dg(select, ll, 1, 1)
    red_out[...] = reduced[: 2 * CW]
    redl[r] = reduced[2 * CW :]

    pl.semaphore_wait(barrier, 31)

    red_copy = pltpu.make_async_remote_copy(
        src_ref=red_out, dst_ref=red_in, send_sem=red_s.at[0], recv_sem=red_r.at[0],
        device_id={"row": (r - x + NROW) % NROW}, device_id_type=MESH,
    )

    @pl.when(x != 0)
    def _():
        red_copy.start()

    @pl.when(x == 0)
    def _():
        red_in[...] = red_out[...]

    def redl_copy(src_row, dst_row):
        return pltpu.make_async_remote_copy(
            src_ref=redl.at[src_row], dst_ref=redl.at[src_row],
            send_sem=redl_s.at[dst_row], recv_sem=redl_r.at[src_row],
            device_id={"row": dst_row}, device_id_type=MESH,
        )

    for k in range(1, NROW):
        redl_copy(r, (r + k) % NROW).start()

    def band(columns, block):
        index = block * NROW + r
        near = jnp.concatenate(
            [
                ids_ref[pl.ds(jnp.maximum(index - 1, 0), 1), :],
                ids_ref[pl.ds(index, 1), :],
                ids_ref[pl.ds(jnp.minimum(index + 1, 63), 1), :],
            ],
            axis=1,
        )
        coef = jnp.zeros(near.shape, F32)
        for k in range(8):
            coef = jnp.where(near == k, kappa_ref[k], coef)
        coef = coef + 4.0
        here = coef[:, Q : 2 * Q]
        before = pltpu.roll(coef, 1, 1)[:, Q : 2 * Q]
        after = pltpu.roll(coef, 3 * Q - 1, 1)[:, Q : 2 * Q]
        row = index * Q + lanes((1, Q))
        ends = jnp.where((row == 0) | (row == 64 * Q - 1), 1.0, 2.0)
        off = row - columns
        return jnp.where(
            off == 0, here * here + ends,
            jnp.where(
                off == 1, -(here + before),
                jnp.where(off == -1, -(here + after), jnp.where(jnp.abs(off) == 2, 1.0, 0.0)),
            ),
        )

    target = node_row // PW * Q + node_row % Q
    top_band = jnp.concatenate(
        [band(own_cols[:CW], 1), band(land_col, 0), band(land_col, 1)], axis=0
    )
    top_band = jnp.where(s == 0, top_band, 0.0)
    own_band = band(own_cols, s)

    @pl.when(x != 0)
    def _():
        red_copy.wait_recv()

    for k in range(1, NROW):
        redl_copy((r + k) % NROW, r).wait_recv()
    reduced_all = jnp.concatenate([red_in[...], redl[0] + redl[1] + redl[2] + redl[3]], axis=0)
    part = -mm(reduced_all, live_hi[...], live_lo[...], 0)
    part_hi, part_lo = split(part)
    pst[...] = jnp.concatenate([part_hi[: 2 * CW], part_lo[: 2 * CW]], axis=0)

    place_top = jnp.where(target == rows_of((2 * Q, 1)), 1.0, 0.0).astype(BF16)
    top = dg(jnp.concatenate([part_hi, part_lo], axis=0), place_top, 1, 1)
    top = top[: 2 * CW + NLAND] + top[2 * CW + NLAND :]
    top_out[...] = top_band + jnp.concatenate(
        [top[:CW, Q:], top[2 * CW :, :Q], top[2 * CW :, Q:]], axis=0
    )

    def top_copy(src_sub, dst_sub):
        return pltpu.make_async_remote_copy(
            src_ref=top_out.at[pl.ds(pl.multiple_of(dst_sub * 8, 8), 8)], dst_ref=top_in.at[src_sub],
            send_sem=top_s.at[dst_sub], recv_sem=top_r.at[src_sub],
            device_id={"sub": dst_sub}, device_id_type=MESH,
        )

    def top_start(k, carry):
        top_copy(s, (s + k) % NSUB).start()
        return carry

    lax.fori_loop(1, NSUB, top_start, 0)

    right = {"sub": (s + 1) % NSUB}
    left = {"sub": (s + NSUB - 1) % NSUB}

    def contribution(block_a, block_b):
        place = rows_of((2 * Q, 1))
        place = jnp.where(place < Q, block_a * Q + place, block_b * Q + place - Q)
        place = jnp.where(target == place, 1.0, 0.0).astype(BF16)
        both = dg(pst[...], place, 1, 1)
        both = both[: 2 * CW] + both[2 * CW :]
        return both[:, :Q], both[:, Q:]

    def ring_copy(src, ring, send, recv, step, chunk, where):
        part_of = pl.ds(chunk * CROWS, CROWS)
        return pltpu.make_async_remote_copy(
            src_ref=src.at[part_of], dst_ref=ring.at[step, part_of],
            send_sem=send.at[step, chunk], recv_sem=recv.at[step, chunk],
            device_id=where, device_id_type=MESH,
        )

    def copy_p(src, step, chunk):
        return ring_copy(src, ring_p, rp_s, rp_r, step, chunk, right)

    def copy_m(src, step, chunk):
        return ring_copy(src, ring_m, rm_s, rm_r, step, chunk, left)

    to_right, to_left = contribution((s + 8) % NSUB, (s + 9) % NSUB)
    first[0] = to_right
    first[1] = to_left
    for chunk in range(CHUNKS):
        copy_p(first.at[0], 0, chunk).start()
        copy_m(first.at[1], 0, chunk).start()

    def ring_step(t, carry):
        to_right, to_left = contribution((s + 8 - t) % NSUB, (s + 9 + t) % NSUB)
        for chunk in range(CHUNKS):
            part_of = pl.ds(chunk * CROWS, CROWS)
            static = slice(chunk * CROWS, (chunk + 1) * CROWS)
            copy_p(ring_p.at[t - 1], t - 1, chunk).wait_recv()
            ring_p[t - 1, part_of, :] += to_right[static]
            copy_p(ring_p.at[t - 1], t, chunk).start()
            copy_m(ring_m.at[t - 1], t - 1, chunk).wait_recv()
            ring_m[t - 1, part_of, :] += to_left[static]
            copy_m(ring_m.at[t - 1], t, chunk).start()
        return carry

    def top_wait(k, carry):
        top_copy((s + k) % NSUB, s).wait_recv()
        return carry

    lax.fori_loop(1, NSUB, top_wait, 0)
    top_in[s] = top_out[pl.ds(pl.multiple_of(s * 8, 8), 8), :]
    top_own[...] = jnp.sum(top_in[...], axis=0)

    def tag_copy(src_sub, dst_sub):
        return pltpu.make_async_remote_copy(
            src_ref=top_own, dst_ref=top_all.at[pl.ds(pl.multiple_of(src_sub * 8, 8), 8)],
            send_sem=tag_s.at[dst_sub], recv_sem=tag_r.at[src_sub],
            device_id={"sub": dst_sub}, device_id_type=MESH,
        )

    def tag_start(k, carry):
        tag_copy(s, (s + k) % NSUB).start()
        return carry

    lax.fori_loop(1, NSUB, tag_start, 0)
    top_all[pl.ds(pl.multiple_of(s * 8, 8), 8), :] = top_own[...]

    lax.fori_loop(1, 3, ring_step, 0)

    def tag_wait(k, carry):
        tag_copy((s + k) % NSUB, s).wait_recv()
        return carry

    lax.fori_loop(1, NSUB, tag_wait, 0)

    def piece(pr, px, ph):
        g = 2 * ((pr + px) % NROW) + ph
        return front_top.at[pr, pl.ds(pl.multiple_of(g * CW, CW), CW)]

    def plane_copy(src_row, src_x, dst_row, dst_x):
        return pltpu.make_async_remote_copy(
            src_ref=top_all.at[pl.ds(0, CW)], dst_ref=piece(src_row, src_x, h),
            send_sem=pla_s.at[dst_row * 4 + dst_x], recv_sem=pla_r.at[src_row * 4 + src_x],
            device_id={"row": dst_row, "col": 2 * dst_x + h}, device_id_type=MESH,
        )

    def fwd_copy(pr, px, src, ph):
        return pltpu.make_async_remote_copy(
            src_ref=src, dst_ref=piece(pr, px, ph),
            send_sem=fwd_s.at[pr * 4 + px], recv_sem=fwd_r.at[pr * 4 + px],
            device_id=other, device_id_type=MESH,
        )

    def rland_copy(src_row, dst_row):
        return pltpu.make_async_remote_copy(
            src_ref=top_all.at[pl.ds(CW, 2 * NLAND)], dst_ref=rland.at[src_row],
            send_sem=rl_s.at[dst_row], recv_sem=rl_r.at[src_row],
            device_id={"row": dst_row}, device_id_type=MESH,
        )

    def plane_start(k, carry):
        pr, px = plane_peer(k)
        plane_copy(r, x, pr, px).start()
        return carry

    lax.fori_loop(1, 16, plane_start, 0)
    for k in range(1, NROW):
        rland_copy(r, (r + k) % NROW).start()
    fwd_copy(r, x, top_all.at[pl.ds(0, CW)], h).start()
    front_top[r, pl.ds(pl.multiple_of(group * CW, CW), CW), :] = top_all[:CW]
    rland[r] = top_all[CW:]

    lax.fori_loop(3, 6, ring_step, 0)

    load_dinv.wait()
    for k in range(2):
        d_hi, d_lo = split(dinv[k])
        gram = dg(d_hi, d_hi, 0, 0) + dg(d_hi, d_lo, 0, 0) + dg(d_lo, d_hi, 0, 0)
        g_hi, g_lo = split(gram)
        s_hi[k] = g_hi
        s_lo[k] = g_lo

    def plane_forward(k, carry):
        pr, px = plane_peer(16 - k)
        plane_copy(pr, px, r, x).wait_recv()
        fwd_copy(pr, px, piece(pr, px, h), h).start()
        return carry

    lax.fori_loop(1, 16, plane_forward, 0)
    lax.fori_loop(6, 7, ring_step, 0)

    to_right, own = contribution((s + 1) % NSUB, s)
    for chunk in range(CHUNKS):
        part_of = pl.ds(chunk * CROWS, CROWS)
        static = slice(chunk * CROWS, (chunk + 1) * CROWS)
        copy_p(ring_p.at[6], 6, chunk).wait_recv()
        ring_p[6, part_of, :] += to_right[static]
        copy_p(ring_p.at[6], 7, chunk).start()
    own = own + own_band
    for chunk in range(CHUNKS):
        part_of = pl.ds(chunk * CROWS, CROWS)
        static = slice(chunk * CROWS, (chunk + 1) * CROWS)
        copy_m(ring_m.at[6], 6, chunk).wait_recv()
        copy_p(ring_p.at[7], 7, chunk).wait_recv()
        fx[group, part_of, :] = own[static] + ring_m[6, part_of, :] + ring_p[7, part_of, :]

    def slot(px, ph):
        return 2 * ((r + px) % NROW) + ph

    def xag_copy(src_x, dst_x):
        return pltpu.make_async_remote_copy(
            src_ref=fx.at[slot(src_x, h)], dst_ref=fx.at[slot(src_x, h)],
            send_sem=xa_s.at[dst_x], recv_sem=xa_r.at[src_x],
            device_id={"col": 2 * dst_x + h}, device_id_type=MESH,
        )

    def xfwd_copy(px, ph):
        return pltpu.make_async_remote_copy(
            src_ref=fx.at[slot(px, ph)], dst_ref=fx.at[slot(px, ph)],
            send_sem=xf_s.at[px], recv_sem=xf_r.at[px],
            device_id=other, device_id_type=MESH,
        )

    for k in range(1, 4):
        xag_copy(x, (x + k) % 4).start()
    xfwd_copy(x, h).start()

    def fwd_wait(k, carry):
        pr, px = k // 4, k % 4
        fwd_copy(pr, px, piece(pr, px, 1 - h), 1 - h).wait_recv()
        return carry

    lax.fori_loop(0, 16, fwd_wait, 0)
    for k in range(1, NROW):
        rland_copy((r + k) % NROW, r).wait_recv()
    f_hi, f_lo = split(jnp.concatenate([front_top[k] for k in range(NROW)], axis=1))
    r0 = jnp.concatenate([rland[k, :NLAND] for k in range(NROW)], axis=1)
    r1 = jnp.concatenate([rland[k, NLAND:] for k in range(NROW)], axis=1)
    own_rows = pl.ds(pl.multiple_of(c * CW, CW), CW)
    d0_own = dinv[0, own_rows, :]
    d1_own = dinv[1, own_rows, :]
    w0 = mm(r0, s_hi[0], s_lo[0], 0)
    t1 = r1 - mm(w0, f_hi, f_lo, 0)
    w1 = mm(t1, s_hi[1], s_lo[1], 0)
    back = mm(jnp.concatenate([d1_own, w1], axis=0), f_hi, f_lo, 1)
    back = mm(back, s_hi[0], s_lo[0], 0)
    column = lanes((NLAND, PW))
    e0 = jnp.where(column == land_col, 1.0, 0.0)
    e1 = jnp.where(column + PW == land_col, 1.0, 0.0)
    left0 = jnp.concatenate([d0_own, -back[:CW], e0 - w0 + back[CW:]], axis=0)
    left1 = jnp.concatenate([d1_own, e1 - w1], axis=0)

    for k in range(1, 4):
        px = (x + k) % 4
        xag_copy(px, x).wait_recv()
        xfwd_copy(px, h).start()
    for k in range(4):
        xfwd_copy(k, 1 - h).wait_recv()
    f0_hi, f0_lo = split(jnp.concatenate([fx[k, :CW] for k in range(NCOL)], axis=0))
    f1_hi, f1_lo = split(jnp.concatenate([fx[k, CW:] for k in range(NCOL)], axis=0))
    out0 = mm(left0, f0_hi, f0_lo, 0)
    out1 = mm(left1, f1_hi, f1_lo, 0)
    row_in = s * PW + r * Q + lanes((CW, Q))
    col_in = c * CW + rows_of((CW, Q))
    pf_ref[:CW] = jnp.where(row_in >= col_in, out0[:CW], 0.0)
    pf_ref[CW:] = jnp.where(row_in - PW >= col_in, out0[CW : 2 * CW] + out1[:CW], 0.0)
    ls_ref[...] = out0[2 * CW :] + out1[CW:]

    own_quarter = pl.ds(pl.multiple_of(r * Q, Q), Q)

    @pl.when(s == 0)
    def _():
        d_hi, d_lo = split(dinv[0, own_quarter, :])
        ls_ref[...] = mm(r0, d_hi, d_lo, 1)

    @pl.when(s == 1)
    def _():
        d_hi, d_lo = split(dinv[1, own_quarter, :])
        ls_ref[...] = mm(t1, d_hi, d_lo, 1)

    @pl.when(x != 0)
    def _():
        red_copy.wait_send()

    for k in range(1, NROW):
        redl_copy(r, (r + k) % NROW).wait_send()
        rland_copy(r, (r + k) % NROW).wait_send()
        xag_copy(x, (x + k) % 4).wait_send()

    def sent_z(k, carry):
        top_copy(s, (s + k) % NSUB).wait_send()
        tag_copy(s, (s + k) % NSUB).wait_send()
        return carry

    lax.fori_loop(1, NSUB, sent_z, 0)

    def sent_plane(k, carry):
        pr, px = plane_peer(k)
        plane_copy(r, x, pr, px).wait_send()
        return carry

    lax.fori_loop(1, 16, sent_plane, 0)

    def sent_fwd(k, carry):
        pr, px = k // 4, k % 4
        fwd_copy(pr, px, piece(pr, px, h), h).wait_send()
        return carry

    lax.fori_loop(0, 16, sent_fwd, 0)
    for k in range(4):
        xfwd_copy(k, h).wait_send()
    for chunk in range(CHUNKS):
        copy_p(first.at[0], 0, chunk).wait_send()
        copy_m(first.at[1], 0, chunk).wait_send()

        def sent_ring(t, carry):
            copy_p(ring_p.at[t - 1], t, chunk).wait_send()
            copy_m(ring_m.at[t - 1], t, chunk).wait_send()
            return carry

        lax.fori_loop(1, 7, sent_ring, 0)
        copy_p(ring_p.at[6], 7, chunk).wait_send()


def on_device(child_factor, child_map, child_len, class_ids, class_kappa, landmarks, diag_inverse):
    vmem = pl.BlockSpec(memory_space=pltpu.VMEM)
    smem = pl.BlockSpec(memory_space=pltpu.SMEM)
    hbm = pl.BlockSpec(memory_space=pl.ANY)
    dma = pltpu.SemaphoreType.DMA
    tile = (2 * CW, Q)
    panel_factor, landmark_solution = pl.pallas_call(
        kernel,
        out_shape=(
            jax.ShapeDtypeStruct((2 * CW, Q), F32),
            jax.ShapeDtypeStruct((NLAND, Q), F32),
        ),
        in_specs=[hbm, vmem, smem, vmem, smem, vmem, hbm],
        out_specs=(vmem, vmem),
        scratch_shapes=[
            pltpu.VMEM((KCH, NODEQ), F32),
            pltpu.VMEM((2, PW, PW), F32),
            pltpu.VMEM((KCH, NODEQ), BF16),
            pltpu.VMEM((KCH, NODEQ), BF16),
            pltpu.VMEM((2 * CW, KCH), F32),
            pltpu.VMEM((2 * CW, KCH), F32),
            pltpu.VMEM((NROW, NLAND, KCH), F32),
            pltpu.VMEM((4 * CW, NODEQ), BF16),
            pltpu.VMEM(tile, F32),
            pltpu.VMEM((NSUB, 8, Q), F32),
            pltpu.VMEM((8, Q), F32),
            pltpu.VMEM(tile, F32),
            pltpu.VMEM((NROW, PW, Q), F32),
            pltpu.VMEM((NROW, 2 * NLAND, Q), F32),
            pltpu.VMEM((2, PW, PW), BF16),
            pltpu.VMEM((2, PW, PW), BF16),
            pltpu.VMEM((2,) + tile, F32),
            pltpu.VMEM((8,) + tile, F32),
            pltpu.VMEM((7,) + tile, F32),
            pltpu.VMEM((NCOL,) + tile, F32),
            dma((2,)), dma((1,)), dma((1,)), dma((NROW,)), dma((NROW,)),
            dma((NSUB,)), dma((NSUB,)), dma((NSUB,)), dma((NSUB,)),
            dma((16,)), dma((16,)), dma((16,)), dma((16,)), dma((NROW,)), dma((NROW,)),
            dma((8, CHUNKS)), dma((8, CHUNKS)), dma((8, CHUNKS)), dma((8, CHUNKS)),
            dma((4,)), dma((4,)), dma((4,)), dma((4,)),
        ],
        compiler_params=pltpu.CompilerParams(
            collective_id=0, has_side_effects=True, vmem_limit_bytes=48 << 20
        ),
    )(
        child_factor, child_map, child_len, class_ids.reshape(64, Q), class_kappa,
        landmarks.reshape(1, 256), diag_inverse,
    )
    return panel_factor.reshape(2, CW, 1, Q), landmark_solution.reshape(NLAND, 1, Q)


def solution(mesh):
    return jax.shard_map(
        on_device,
        mesh=mesh,
        in_specs=(P("sub", None, "row"), P("sub", None), P("sub"), P(), P(), P(), P()),
        out_specs=(P(None, "col", "sub", "row"), P("col", "sub", "row")),
        check_vma=False,
    )
```

time: 514 us -> 78.2 us (0.15)
  waiting for transfers between devices: 407 us -> 0 us
  Pallas kernels: 0 us -> 69.9 us
  blocking collectives: 65.8 us -> 0 us
  matrix products: 17.6 us -> 0 us
  between operations: 15 us -> 1.3 us
    psum x2 -> x0, waiting for transfers between devices: 257 us -> none  [from_root(): return lax.psum(jnp.where(mine, value, jnp.zeros_like(value)), axis)]
    reduce_scatter x2 -> x0, waiting for transfers between devices: 79.6 us -> none  [the longest x1 58 us: on_device(): lax.psum_scatter(contribution, 'sub', scatter_dimension=1, tiled=True)]
    all_gather x2 -> x0, waiting for transfers between devices: 70.3 us -> none  [the longest x1 43.3 us: on_device(): lax.all_gather(live_factor, 'row', axis=1, tiled=True)]
    pallas_call x0 -> x1, Pallas kernels: none -> 69.9 us  [on_device(): pl.pallas_call(kernel, out_shape=(jax.ShapeDtypeStruct((2 * CW, Q), F32),...]
    all_gather x4 -> x0, blocking collectives: 65.8 us -> none  [the longest x2 46.8 us: on_device(): lax.all_gather(column_slabs[panel_index], 'col', axis=0, tiled=True)]
    dot_general x11 -> x0, matrix products: 17.6 us -> none  [the longest x9 13.9 us: contract(): lax.dot_general(left_part, right_part, (((left_dim,), (right_dim,)), ((),...]
    unnamed x17 -> x14, local copies, waits for them, and re-layouts: 0.75 us -> 6.65 us
  transfers between devices with their start and end apart: 6 -> 0, of which waited for: 6 -> 0; matrix products, arithmetic and copies ran while one was open for 2% -> 0% of each run, Pallas kernels for 0% -> 0%
where the time goes in v1:
time: 78.2 us; the launch traced here: 77.9 us
  Pallas kernels  69.9 us (89%)
  local copies, waits for them, and re-layouts  6.65 us (9%)
  between operations  1.3 us (2%)
    pallas_call x1, Pallas kernels, on_device(): pl.pallas_call(kernel, out_shape=(jax.ShapeDtypeStruct((2 * CW, Q), F32),...  69.9 us
    unnamed x14, local copies, waits for them, and re-layouts  6.65 us

profile of v1, /device:TPU:1, one launch (start us, length us, event | category | flops | bytes accessed | tf_op | source)
XLA Modules:
  0.0 77.9 jit_solution(9758549862366072701)
XLA Ops:
  1.3 0.0 copy-start
  1.3 1.6 %copy-done = f32[2,512,512]{2,1,0:T(8,128)S(1)} copy-done((f32[2,512,512]{2,1,0:T(8,128)S(1)}, f32[2,512,512]{2,1,0:T(8,128)}, u32[]{:S(2)}) %copy-start) | copy-done | bytes 2097176
  2.9 0.0 copy-start.1
  2.9 1.0 %copy-done.1 = f32[1,256,512]{2,1,0:T(8,128)S(1)} copy-done((f32[1,256,512]{2,1,0:T(8,128)S(1)}, f32[1,256,512]{2,1,0:T(8,128)}, u32[]{:S(2)}) %copy-start.1) | copy-done | bytes 524312
  3.9 0.0 copy-start.2
  3.9 0.8 copy-done.2
  4.7 0.0 copy-start.3
  4.7 0.7 copy-done.3
  5.4 0.0 copy-start.4
  5.4 0.7 copy-done.4
  6.0 0.0 copy-start.5
  6.0 0.7 copy-done.5
  6.7 69.9 %shard_map.86 = (f32[128,128]{1,0:T(8,128)S(1)}, f32[32,128]{1,0:T(8,128)S(1)}) custom-call(f32[1,256,512]{2,1,0:T(8,128)S(1)} %copy-done.1, s32[1,2048]{1,0:T(1,128)S(1)} %copy-done.3, s32[1]{0:T(128)S(6)} %copy.13.len_ref, s32[64,128]{1,0:T(8,128)S(1)} %bitcast.9, f32[8]{0:T(128)S(1)} %copy-done.5, s32[1,256]{1,0:T(1,128)S(1)} %bitcast.11, ...), custom_call_target="tpu_custom_call" | custom-call | tf_op jit(solution)/shard_map/pallas_call | solution.py:463
  76.6 0.6 copy.14
  77.3 0.6 copy.15
Async XLA Ops:
  1.3 1.6 %copy-start = (f32[2,512,512]{2,1,0:T(8,128)S(1)}, f32[2,512,512]{2,1,0:T(8,128)}, u32[]{:S(2)}) copy-start(f32[2,512,512]{2,1,0:T(8,128)} %dinv_hbm.1) | copy-start | bytes 6291460
  2.9 1.0 %copy-start.1 = (f32[1,256,512]{2,1,0:T(8,128)S(1)}, f32[1,256,512]{2,1,0:T(8,128)}, u32[]{:S(2)}) copy-start(f32[1,256,512]{2,1,0:T(8,128)} %factor_hbm.1) | copy-start | bytes 1572868
  3.9 0.8 copy-start.2
  4.7 0.7 copy-start.3
  5.4 0.7 copy-start.4
  6.0 0.7 copy-start.5

commit v2 on v1

v2 whole, which is shorter than its diff:
```python
import jax
import jax.numpy as jnp
from jax import lax
from jax.experimental import pallas as pl
from jax.experimental.pallas import tpu as pltpu
from jax.sharding import PartitionSpec as P

F32 = jnp.float32
BF16 = jnp.bfloat16
MESH = pl.DeviceIdType.MESH

NSUB, NROW, NCOL = 16, 4, 8
NEAR = 4
PW, Q, CW, KCH, NODEQ, NLAND = 512, 128, 64, 256, 512, 32
CHUNKS = 2
CROWS = 2 * CW // CHUNKS


def dg(a, b, ca, cb):
    return lax.dot_general(a, b, (((ca,), (cb,)), ((), ())), preferred_element_type=F32)


def split(x):
    hi = x.astype(BF16)
    return hi, (x - hi.astype(F32)).astype(BF16)


def mm(a, b_hi, b_lo, cb):
    n = a.shape[0]
    a_hi, a_lo = split(a)
    both = dg(jnp.concatenate([a_hi, a_lo], axis=0), b_hi, 1, cb)
    return both[:n] + both[n:] + dg(a_hi, b_lo, 1, cb)


def mod(a, n):
    return lax.rem(a, jnp.int32(n))


def lanes(shape):
    return lax.broadcasted_iota(jnp.int32, shape, 1)


def rows_of(shape):
    return lax.broadcasted_iota(jnp.int32, shape, 0)


def kernel(
    factor_hbm, map_hbm, len_hbm, ids_hbm, kappa_hbm, land_hbm, dinv_hbm,
    pf_ref, ls_ref,
    map_ref, len_ref, ids_ref, kappa_ref, land_ref, factor, dinv, live_hi, live_lo, red_out, red_in, redl, pst,
    top_out, near_in, near_sum, far_in, near_all, top_all, front_top, rland, s_hi, s_lo,
    first, ring_p, ring_m, fx,
    ld_sem, red_s, red_r, redl_s, redl_r, near_s, near_r, far_s, far_r, all_s, all_r,
    fy_s, fy_r, fx_s, fx_r, fwd_s, fwd_r, rl_s, rl_r,
    rp_s, rp_r, rm_s, rm_r, xa_s, xa_r, xf_s, xf_r,
):
    s = lax.axis_index("sub")
    r = lax.axis_index("row")
    c = lax.axis_index("col")
    x, h = lax.div(c, 2), mod(c, 2)
    far, near = lax.div(s, NEAR), mod(s, NEAR)
    other = {"col": 2 * x + 1 - h}
    group = 2 * mod(r + x, NROW) + h
    right = {"sub": mod(s + 1, NSUB)}
    left = {"sub": mod(s + NSUB - 1, NSUB)}

    def near_id(k):
        return {"sub": far * NEAR + mod(near + k, NEAR)}

    def far_id(k):
        return {"sub": mod(s + k * NEAR, NSUB)}

    def row_id(k):
        return {"row": mod(r + k, NROW)}

    def x_id(k):
        return {"col": 2 * mod(x + k, 4) + h}

    def remote(src, dst, send, recv, where):
        return pltpu.make_async_remote_copy(
            src_ref=src, dst_ref=dst, send_sem=send, recv_sem=recv, device_id=where, device_id_type=MESH
        )

    three = pl.ds(0, 3)
    of_redl, of_near, of_far = redl.at[three], near_in.at[three], far_in.at[three]
    of_all, of_row, of_rland = top_all.at[pl.ds(0, 3 * 2 * CW // NEAR)], front_top.at[0, 0, three], rland.at[three]

    def arrived(bytes_of, sem):
        remote(bytes_of, bytes_of, sem, sem, other).wait_recv()

    def departed(bytes_of, sem):
        remote(bytes_of, bytes_of, sem, sem, other).wait_send()

    load_factor = pltpu.make_async_copy(factor_hbm.at[0], factor, ld_sem.at[0])
    load_factor.start()
    small = [
        pltpu.make_async_copy(src, dst, ld_sem.at[2 + k])
        for k, (src, dst) in enumerate(
            [(map_hbm, map_ref), (land_hbm, land_ref), (len_hbm, len_ref), (ids_hbm, ids_ref), (kappa_hbm, kappa_ref)]
        )
    ]
    for copy in small:
        copy.start()
    load_dinv = pltpu.make_async_copy(dinv_hbm, dinv, ld_sem.at[1])
    load_dinv.start()
    barrier = pltpu.get_barrier_semaphore()

    for peer in [right, left, other] + [make(k) for make in (near_id, far_id, row_id, x_id) for k in (1, 2, 3)]:
        pl.semaphore_signal(barrier, inc=1, device_id=peer, device_id_type=MESH)

    for copy in small:
        copy.wait()
    node_row = map_ref[:, pl.ds(pl.multiple_of(r * NODEQ, NODEQ), NODEQ)]
    land_row = land_ref[...]
    land_col = jnp.sum(
        jnp.where(lanes((NLAND, 256)) == rows_of((NLAND, 256)) + c * NLAND, land_row.astype(F32), 0.0),
        axis=1, keepdims=True,
    ).astype(jnp.int32)
    iota_col = rows_of((2 * CW, 1))
    send_cols = iota_col // CW * PW + (2 * r + h) * CW + iota_col % CW
    own_cols = iota_col // CW * PW + group * CW + iota_col % CW
    select = jnp.concatenate([send_cols, land_col], axis=0) == node_row
    select = jnp.where(select, 1.0, 0.0).astype(BF16)
    load_factor.wait()
    live = jnp.where(lanes((KCH, NODEQ)) + r * NODEQ < len_ref[0], factor[...], 0.0)
    lh, ll = split(live)
    live_hi[...] = lh
    live_lo[...] = ll
    reduced = dg(select, lh, 1, 1) + dg(select, ll, 1, 1)
    red_out[...] = reduced[: 2 * CW]
    redl[r] = reduced[2 * CW :]

    pl.semaphore_wait(barrier, 15)

    red_copy = remote(red_out, red_in, red_s.at[0], red_r.at[0], {"row": mod(r - x + NROW, NROW)})

    @pl.when(x != 0)
    def _():
        red_copy.start()

    @pl.when(x == 0)
    def _():
        red_in[...] = red_out[...]

    redl_copies = [remote(redl.at[r], redl.at[r], redl_s, redl_r, row_id(k)) for k in (1, 2, 3)]
    for copy in redl_copies:
        copy.start()

    def band(columns, block):
        index = block * NROW + r
        near = jnp.concatenate(
            [
                ids_ref[pl.ds(jnp.maximum(index - 1, 0), 1), :],
                ids_ref[pl.ds(index, 1), :],
                ids_ref[pl.ds(jnp.minimum(index + 1, 63), 1), :],
            ],
            axis=1,
        )
        coef = jnp.zeros(near.shape, F32)
        for k in range(8):
            coef = jnp.where(near == k, kappa_ref[k], coef)
        coef = coef + 4.0
        here = coef[:, Q : 2 * Q]
        before = pltpu.roll(coef, 1, 1)[:, Q : 2 * Q]
        after = pltpu.roll(coef, 3 * Q - 1, 1)[:, Q : 2 * Q]
        row = index * Q + lanes((1, Q))
        ends = jnp.where((row == 0) | (row == 64 * Q - 1), 1.0, 2.0)
        off = row - columns
        return jnp.where(
            off == 0, here * here + ends,
            jnp.where(
                off == 1, -(here + before),
                jnp.where(off == -1, -(here + after), jnp.where(jnp.abs(off) == 2, 1.0, 0.0)),
            ),
        )

    load_dinv.wait()
    for k in range(2):
        d_hi, d_lo = split(dinv[k])
        gram = dg(d_hi, d_hi, 0, 0) + dg(d_hi, d_lo, 0, 0) + dg(d_lo, d_hi, 0, 0)
        g_hi, g_lo = split(gram)
        s_hi[k] = g_hi
        s_lo[k] = g_lo

    target = node_row // PW * Q + node_row % Q
    top_band = jnp.concatenate(
        [band(own_cols[:CW], 1), band(land_col, 0), band(land_col, 1)], axis=0
    )
    top_band = jnp.where(s == 0, top_band, 0.0)
    own_band = band(own_cols, s)

    @pl.when(x != 0)
    def _():
        red_copy.wait_recv()

    arrived(of_redl, redl_r)
    reduced_all = jnp.concatenate([red_in[...], redl[0] + redl[1] + redl[2] + redl[3]], axis=0)
    part = -mm(reduced_all, live_hi[...], live_lo[...], 0)
    part_hi, part_lo = split(part)
    pst[...] = jnp.concatenate([part_hi[: 2 * CW], part_lo[: 2 * CW]], axis=0)

    place_top = jnp.where(target == rows_of((2 * Q, 1)), 1.0, 0.0).astype(BF16)
    top = dg(jnp.concatenate([part_hi, part_lo], axis=0), place_top, 1, 1)
    top = top[: 2 * CW + NLAND] + top[2 * CW + NLAND :]
    top_out[...] = top_band + jnp.concatenate(
        [top[:CW, Q:], top[2 * CW :, :Q], top[2 * CW :, Q:]], axis=0
    )

    near_rows = 2 * CW // NEAR

    def quarter_rows(k):
        return pl.ds(pl.multiple_of(k * near_rows, near_rows), near_rows)

    near_copies = [
        remote(top_out.at[quarter_rows(mod(near + k, NEAR))], near_in.at[near], near_s, near_r, near_id(k))
        for k in (1, 2, 3)
    ]
    for copy in near_copies:
        copy.start()
    near_in[near] = top_out[quarter_rows(near), :]

    def contribution(block_a, block_b):
        place = rows_of((2 * Q, 1))
        place = jnp.where(place < Q, block_a * Q + place, block_b * Q + place - Q)
        place = jnp.where(target == place, 1.0, 0.0).astype(BF16)
        both = dg(pst[...], place, 1, 1)
        both = both[: 2 * CW] + both[2 * CW :]
        return both[:, :Q], both[:, Q:]

    def ring_copy(src, ring, send, recv, step, chunk, where):
        part_of = pl.ds(chunk * CROWS, CROWS)
        return pltpu.make_async_remote_copy(
            src_ref=src.at[part_of], dst_ref=ring.at[step, part_of],
            send_sem=send.at[step, chunk], recv_sem=recv.at[step, chunk],
            device_id=where, device_id_type=MESH,
        )

    def copy_p(src, step, chunk):
        return ring_copy(src, ring_p, rp_s, rp_r, step, chunk, right)

    def copy_m(src, step, chunk):
        return ring_copy(src, ring_m, rm_s, rm_r, step, chunk, left)

    to_right, to_left = contribution(mod(s + 8, NSUB), mod(s + 9, NSUB))
    first[0] = to_right
    first[1] = to_left
    for chunk in range(CHUNKS):
        copy_p(first.at[0], 0, chunk).start()
        copy_m(first.at[1], 0, chunk).start()

    def ring_step(t, carry):
        to_right, to_left = contribution(mod(s + 8 - t, NSUB), mod(s + 9 + t, NSUB))
        for chunk in range(CHUNKS):
            part_of = pl.ds(chunk * CROWS, CROWS)
            static = slice(chunk * CROWS, (chunk + 1) * CROWS)
            copy_p(ring_p.at[t - 1], t - 1, chunk).wait_recv()
            ring_p[t - 1, part_of, :] += to_right[static]
            copy_p(ring_p.at[t - 1], t, chunk).start()
            copy_m(ring_m.at[t - 1], t - 1, chunk).wait_recv()
            ring_m[t - 1, part_of, :] += to_left[static]
            copy_m(ring_m.at[t - 1], t, chunk).start()
        return carry

    lax.fori_loop(1, 2, ring_step, 0)
    arrived(of_near, near_r)
    near_sum[...] = near_in[0] + near_in[1] + near_in[2] + near_in[3]
    far_copies = [remote(near_sum, far_in.at[far], far_s, far_r, far_id(k)) for k in (1, 2, 3)]
    for copy in far_copies:
        copy.start()
    far_in[far] = near_sum[...]

    lax.fori_loop(2, 3, ring_step, 0)
    arrived(of_far, far_r)
    near_all[...] = far_in[0] + far_in[1] + far_in[2] + far_in[3]
    all_copies = [remote(near_all, top_all.at[quarter_rows(near)], all_s, all_r, near_id(k)) for k in (1, 2, 3)]
    for copy in all_copies:
        copy.start()
    top_all[quarter_rows(near), :] = near_all[...]

    lax.fori_loop(3, 4, ring_step, 0)
    arrived(of_all, all_r)

    row_copies = [remote(top_all.at[pl.ds(0, CW)], front_top.at[h, x, r], fy_s, fy_r, row_id(k)) for k in (1, 2, 3)]
    rland_copies = [
        remote(top_all.at[pl.ds(CW, 2 * NLAND)], rland.at[r], rl_s, rl_r, row_id(k)) for k in (1, 2, 3)
    ]
    for copy in row_copies + rland_copies:
        copy.start()
    front_top[h, x, r] = top_all[:CW]
    rland[r] = top_all[CW:]

    def x_copy(src_x, dst_x, where):
        return remote(front_top.at[h, src_x], front_top.at[h, src_x], fx_s.at[dst_x], fx_r.at[src_x], where)

    def fwd_copy(src_x, core):
        return remote(front_top.at[core, src_x], front_top.at[core, src_x], fwd_s.at[src_x], fwd_r.at[src_x], other)

    lax.fori_loop(4, 5, ring_step, 0)
    arrived(of_row, fy_r)
    x_copies = [x_copy(x, mod(x + k, 4), x_id(k)) for k in (1, 2, 3)]
    for copy in x_copies:
        copy.start()
    fwd_copy(x, h).start()

    lax.fori_loop(5, 7, ring_step, 0)
    for k in (1, 3, 2):
        from_x = mod(x + k, 4)
        x_copy(from_x, x, other).wait_recv()
        fwd_copy(from_x, h).start()

    to_right, own = contribution(mod(s + 1, NSUB), s)
    for chunk in range(CHUNKS):
        part_of = pl.ds(chunk * CROWS, CROWS)
        static = slice(chunk * CROWS, (chunk + 1) * CROWS)
        copy_p(ring_p.at[6], 6, chunk).wait_recv()
        ring_p[6, part_of, :] += to_right[static]
        copy_p(ring_p.at[6], 7, chunk).start()
    own = own + own_band
    for chunk in range(CHUNKS):
        part_of = pl.ds(chunk * CROWS, CROWS)
        static = slice(chunk * CROWS, (chunk + 1) * CROWS)
        copy_m(ring_m.at[6], 6, chunk).wait_recv()
        copy_p(ring_p.at[7], 7, chunk).wait_recv()
        fx[group, part_of, :] = own[static] + ring_m[6, part_of, :] + ring_p[7, part_of, :]

    def slot(px, ph):
        return 2 * mod(r + px, NROW) + ph

    def xag_copy(src_x, dst_x, where):
        return remote(fx.at[slot(src_x, h)], fx.at[slot(src_x, h)], xa_s.at[dst_x], xa_r.at[src_x], where)

    def xfwd_copy(px, ph):
        return remote(fx.at[slot(px, ph)], fx.at[slot(px, ph)], xf_s.at[px], xf_r.at[px], other)

    xag_copies = [xag_copy(x, mod(x + k, 4), x_id(k)) for k in (1, 2, 3)]
    for copy in xag_copies:
        copy.start()
    xfwd_copy(x, h).start()

    for k in range(4):
        fwd_copy(k, 1 - h).wait_recv()
    arrived(of_rland, rl_r)
    f_hi, f_lo = split(
        jnp.concatenate(
            [
                jnp.concatenate([front_top[g % 2, (g // 2 - k) % 4, k] for g in range(NCOL)], axis=0)
                for k in range(NROW)
            ],
            axis=1,
        )
    )
    r0 = jnp.concatenate([rland[k, :NLAND] for k in range(NROW)], axis=1)
    r1 = jnp.concatenate([rland[k, NLAND:] for k in range(NROW)], axis=1)
    own_rows = pl.ds(pl.multiple_of(c * CW, CW), CW)
    d0_own = dinv[0, own_rows, :]
    d1_own = dinv[1, own_rows, :]
    w0 = mm(r0, s_hi[0], s_lo[0], 0)
    t1 = r1 - mm(w0, f_hi, f_lo, 0)
    w1 = mm(t1, s_hi[1], s_lo[1], 0)
    back = mm(jnp.concatenate([d1_own, w1], axis=0), f_hi, f_lo, 1)
    back = mm(back, s_hi[0], s_lo[0], 0)
    column = lanes((NLAND, PW))
    e0 = jnp.where(column == land_col, 1.0, 0.0)
    e1 = jnp.where(column + PW == land_col, 1.0, 0.0)
    left0 = jnp.concatenate([d0_own, -back[:CW], e0 - w0 + back[CW:]], axis=0)
    left1 = jnp.concatenate([d1_own, e1 - w1], axis=0)

    for k in (1, 3, 2):
        from_x = mod(x + k, 4)
        xag_copy(from_x, x, other).wait_recv()
        xfwd_copy(from_x, h).start()
    for k in range(4):
        xfwd_copy(k, 1 - h).wait_recv()
    f0_hi, f0_lo = split(jnp.concatenate([fx[k, :CW] for k in range(NCOL)], axis=0))
    f1_hi, f1_lo = split(jnp.concatenate([fx[k, CW:] for k in range(NCOL)], axis=0))
    out0 = mm(left0, f0_hi, f0_lo, 0)
    out1 = mm(left1, f1_hi, f1_lo, 0)
    row_in = s * PW + r * Q + lanes((CW, Q))
    col_in = c * CW + rows_of((CW, Q))
    pf_ref[:CW] = jnp.where(row_in >= col_in, out0[:CW], 0.0)
    pf_ref[CW:] = jnp.where(row_in - PW >= col_in, out0[CW : 2 * CW] + out1[:CW], 0.0)
    ls_ref[...] = out0[2 * CW :] + out1[CW:]

    own_quarter = pl.ds(pl.multiple_of(r * Q, Q), Q)

    @pl.when(s == 0)
    def _():
        d_hi, d_lo = split(dinv[0, own_quarter, :])
        ls_ref[...] = mm(r0, d_hi, d_lo, 1)

    @pl.when(s == 1)
    def _():
        d_hi, d_lo = split(dinv[1, own_quarter, :])
        ls_ref[...] = mm(t1, d_hi, d_lo, 1)

    @pl.when(x != 0)
    def _():
        red_copy.wait_send()

    for bytes_of, sem in (
        (of_redl, redl_s), (of_near, near_s), (of_far, far_s), (of_all, all_s), (of_row, fy_s), (of_rland, rl_s)
    ):
        departed(bytes_of, sem)
    for copy in x_copies + xag_copies:
        copy.wait_send()
    for k in range(4):
        fwd_copy(k, h).wait_send()
    for k in range(4):
        xfwd_copy(k, h).wait_send()
    for chunk in range(CHUNKS):
        copy_p(first.at[0], 0, chunk).wait_send()
        copy_m(first.at[1], 0, chunk).wait_send()

        def sent_ring(t, carry):
            copy_p(ring_p.at[t - 1], t, chunk).wait_send()
            copy_m(ring_m.at[t - 1], t, chunk).wait_send()
            return carry

        lax.fori_loop(1, 7, sent_ring, 0)
        copy_p(ring_p.at[6], 7, chunk).wait_send()


def on_device(child_factor, child_map, child_len, class_ids, class_kappa, landmarks, diag_inverse):
    vmem = pl.BlockSpec(memory_space=pltpu.VMEM)
    hbm = pl.BlockSpec(memory_space=pltpu.HBM)
    dma = pltpu.SemaphoreType.DMA
    tile = (2 * CW, Q)
    panel_factor, landmark_solution = pl.pallas_call(
        kernel,
        out_shape=(
            jax.ShapeDtypeStruct((2 * CW, Q), F32),
            jax.ShapeDtypeStruct((NLAND, Q), F32),
        ),
        in_specs=[hbm] * 7,
        out_specs=(vmem, vmem),
        scratch_shapes=[
            pltpu.VMEM((1, NROW * NODEQ), jnp.int32),
            pltpu.SMEM((1,), jnp.int32),
            pltpu.VMEM((64, Q), jnp.int32),
            pltpu.SMEM((8,), F32),
            pltpu.VMEM((1, 256), jnp.int32),
            pltpu.VMEM((KCH, NODEQ), F32),
            pltpu.VMEM((2, PW, PW), F32),
            pltpu.VMEM((KCH, NODEQ), BF16),
            pltpu.VMEM((KCH, NODEQ), BF16),
            pltpu.VMEM((2 * CW, KCH), F32),
            pltpu.VMEM((2 * CW, KCH), F32),
            pltpu.VMEM((NROW, NLAND, KCH), F32),
            pltpu.VMEM((4 * CW, NODEQ), BF16),
            pltpu.VMEM(tile, F32),
            pltpu.VMEM((NEAR, 2 * CW // NEAR, Q), F32),
            pltpu.VMEM((2 * CW // NEAR, Q), F32),
            pltpu.VMEM((NEAR, 2 * CW // NEAR, Q), F32),
            pltpu.VMEM((2 * CW // NEAR, Q), F32),
            pltpu.VMEM(tile, F32),
            pltpu.VMEM((2, 4, NROW, CW, Q), F32),
            pltpu.VMEM((NROW, 2 * NLAND, Q), F32),
            pltpu.VMEM((2, PW, PW), BF16),
            pltpu.VMEM((2, PW, PW), BF16),
            pltpu.VMEM((2,) + tile, F32),
            pltpu.VMEM((8,) + tile, F32),
            pltpu.VMEM((7,) + tile, F32),
            pltpu.VMEM((NCOL,) + tile, F32),
            dma((7,)), dma((1,)), dma((1,)), dma, dma,
            dma, dma, dma, dma, dma, dma,
            dma, dma, dma((4,)), dma((4,)), dma((4,)), dma((4,)), dma, dma,
            dma((8, CHUNKS)), dma((8, CHUNKS)), dma((8, CHUNKS)), dma((8, CHUNKS)),
            dma((4,)), dma((4,)), dma((4,)), dma((4,)),
        ],
        compiler_params=pltpu.CompilerParams(
            collective_id=0, has_side_effects=True, vmem_limit_bytes=63 << 20
        ),
    )(
        child_factor, child_map, child_len, class_ids.reshape(64, Q), class_kappa,
        landmarks.reshape(1, 256), diag_inverse,
    )
    return panel_factor.reshape(2, CW, 1, Q), landmark_solution.reshape(NLAND, 1, Q)


def solution(mesh):
    return jax.shard_map(
        on_device,
        mesh=mesh,
        in_specs=(P("sub", None, "row"), P("sub", None), P("sub"), P(), P(), P(), P()),
        out_specs=(P(None, "col", "sub", "row"), P("col", "sub", "row")),
        check_vma=False,
    )
```

time: 78.2 us -> 68.5 us (0.88)
  Pallas kernels: 69.9 us -> 64.2 us
  local copies, waits for them, and re-layouts: 6.65 us -> 2.8 us
    pallas_call x1, Pallas kernels: 69.9 us -> 64.2 us  [on_device(): pl.pallas_call(kernel, out_shape=(jax.ShapeDtypeStruct((2 * CW, Q), F32),...]
    unnamed x14 -> x2, local copies, waits for them, and re-layouts: 6.65 us -> 2.8 us
where the time goes in v2:
time: 68.5 us; the launch traced here: 68.3 us
  Pallas kernels  64.2 us (94%)
  local copies, waits for them, and re-layouts  2.8 us (4%)
  between operations  1.29 us (2%)
    pallas_call x1, Pallas kernels, on_device(): pl.pallas_call(kernel, out_shape=(jax.ShapeDtypeStruct((2 * CW, Q), F32),...  64.2 us
    unnamed x2, local copies, waits for them, and re-layouts  2.8 us

profile of v2, /device:TPU:1, one launch (start us, length us, event | category | flops | bytes accessed | tf_op | source)
XLA Modules:
  0.0 68.3 jit_solution(7090420861518469207)
XLA Ops:
  1.3 64.2 %shard_map.86 = (f32[128,128]{1,0:T(8,128)}, f32[32,128]{1,0:T(8,128)}) custom-call(f32[1,256,512]{2,1,0:T(8,128)} %factor_hbm.1, s32[1,2048]{1,0:T(1,128)} %map_hbm.1, s32[1]{0:T(128)S(6)} %copy.13.len_hbm, s32[64,128]{1,0:T(8,128)} %bitcast.9, f32[8]{0:T(128)} %kappa_hbm.1, s32[1,256]{1,0:T(1,128)} %bitcast.11, f32[2,512,512]{2,1,0:T(8,128)} %dinv_hbm.1), custom_call_target="tpu_custom_call" | custom-call | tf_op jit(solution)/shard_map/pallas_call | solution.py:428
  65.5 1.5 %copy.14 = f32[2,64,1,128]{3,2,1,0:T(1,128)} copy(f32[2,64,1,128]{3,2,1,0:T(1,128)} %bitcast.8) | data formatting | bytes 131072
  66.9 1.3 %copy.15 = f32[32,1,128]{2,1,0:T(1,128)} copy(f32[32,1,128]{2,1,0:T(1,128)} %bitcast.10) | data formatting | bytes 32768

commit v3 on v2

--- a/solution.py
+++ b/solution.py
@@ -11,6 +11,7 @@
 
 NSUB, NROW, NCOL = 16, 4, 8
 NEAR = 4
+ORDER = (1, 4, 5, 6, 7)
 PW, Q, CW, KCH, NODEQ, NLAND = 512, 128, 64, 256, 512, 32
 CHUNKS = 2
 CROWS = 2 * CW // CHUNKS
@@ -46,7 +47,7 @@
 
 def kernel(
     factor_hbm, map_hbm, len_hbm, ids_hbm, kappa_hbm, land_hbm, dinv_hbm,
-    pf_ref, ls_ref,
+    out_ref,
     map_ref, len_ref, ids_ref, kappa_ref, land_ref, factor, dinv, live_hi, live_lo, red_out, red_in, redl, pst,
     top_out, near_in, near_sum, far_in, near_all, top_all, front_top, rland, s_hi, s_lo,
     first, ring_p, ring_m, fx,
@@ -261,33 +262,12 @@
             copy_m(ring_m.at[t - 1], t, chunk).start()
         return carry
 
-    lax.fori_loop(1, 2, ring_step, 0)
-    arrived(of_near, near_r)
-    near_sum[...] = near_in[0] + near_in[1] + near_in[2] + near_in[3]
     far_copies = [remote(near_sum, far_in.at[far], far_s, far_r, far_id(k)) for k in (1, 2, 3)]
-    for copy in far_copies:
-        copy.start()
-    far_in[far] = near_sum[...]
-
-    lax.fori_loop(2, 3, ring_step, 0)
-    arrived(of_far, far_r)
-    near_all[...] = far_in[0] + far_in[1] + far_in[2] + far_in[3]
     all_copies = [remote(near_all, top_all.at[quarter_rows(near)], all_s, all_r, near_id(k)) for k in (1, 2, 3)]
-    for copy in all_copies:
-        copy.start()
-    top_all[quarter_rows(near), :] = near_all[...]
-
-    lax.fori_loop(3, 4, ring_step, 0)
-    arrived(of_all, all_r)
-
     row_copies = [remote(top_all.at[pl.ds(0, CW)], front_top.at[h, x, r], fy_s, fy_r, row_id(k)) for k in (1, 2, 3)]
     rland_copies = [
         remote(top_all.at[pl.ds(CW, 2 * NLAND)], rland.at[r], rl_s, rl_r, row_id(k)) for k in (1, 2, 3)
     ]
-    for copy in row_copies + rland_copies:
-        copy.start()
-    front_top[h, x, r] = top_all[:CW]
-    rland[r] = top_all[CW:]
 
     def x_copy(src_x, dst_x, where):
         return remote(front_top.at[h, src_x], front_top.at[h, src_x], fx_s.at[dst_x], fx_r.at[src_x], where)
@@ -295,18 +275,50 @@
     def fwd_copy(src_x, core):
         return remote(front_top.at[core, src_x], front_top.at[core, src_x], fwd_s.at[src_x], fwd_r.at[src_x], other)
 
-    lax.fori_loop(4, 5, ring_step, 0)
-    arrived(of_row, fy_r)
     x_copies = [x_copy(x, mod(x + k, 4), x_id(k)) for k in (1, 2, 3)]
-    for copy in x_copies:
-        copy.start()
-    fwd_copy(x, h).start()
-
-    lax.fori_loop(5, 7, ring_step, 0)
-    for k in (1, 3, 2):
-        from_x = mod(x + k, 4)
-        x_copy(from_x, x, other).wait_recv()
-        fwd_copy(from_x, h).start()
+
+    def near_step():
+        arrived(of_near, near_r)
+        near_sum[...] = near_in[0] + near_in[1] + near_in[2] + near_in[3]
+        for copy in far_copies:
+            copy.start()
+        far_in[far] = near_sum[...]
+
+    def far_step():
+        arrived(of_far, far_r)
+        near_all[...] = far_in[0] + far_in[1] + far_in[2] + far_in[3]
+        for copy in all_copies:
+            copy.start()
+        top_all[quarter_rows(near), :] = near_all[...]
+
+    def all_step():
+        arrived(of_all, all_r)
+        for copy in row_copies + rland_copies:
+            copy.start()
+        front_top[h, x, r] = top_all[:CW]
+        rland[r] = top_all[CW:]
+
+    def row_step():
+        arrived(of_row, fy_r)
+        for copy in x_copies:
+            copy.start()
+        fwd_copy(x, h).start()
+
+    def x_step():
+        for k in (1, 3, 2):
+            from_x = mod(x + k, 4)
+            x_copy(from_x, x, other).wait_recv()
+            fwd_copy(from_x, h).start()
+
+    done = 1
+    for top_step, ring_done in zip((near_step, far_step, all_step, row_step, x_step), ORDER):
+        if min(ring_done, 6) >= done:
+            lax.fori_loop(done, min(ring_done, 6) + 1, ring_step, 0)
+            done = min(ring_done, 6) + 1
+        if ring_done < 7:
+            top_step()
+    if done < 7:
+        lax.fori_loop(done, 7, ring_step, 0)
 
     to_right, own = contribution(mod(s + 1, NSUB), s)
     for chunk in range(CHUNKS):
@@ -336,6 +348,10 @@
     for copy in xag_copies:
         copy.start()
     xfwd_copy(x, h).start()
+
+    for top_step, ring_done in zip((near_step, far_step, all_step, row_step, x_step), ORDER):
+        if ring_done == 7:
+            top_step()
 
     for k in range(4):
         fwd_copy(k, 1 - h).wait_recv()
@@ -377,21 +393,21 @@
     out1 = mm(left1, f1_hi, f1_lo, 0)
     row_in = s * PW + r * Q + lanes((CW, Q))
     col_in = c * CW + rows_of((CW, Q))
-    pf_ref[:CW] = jnp.where(row_in >= col_in, out0[:CW], 0.0)
-    pf_ref[CW:] = jnp.where(row_in - PW >= col_in, out0[CW : 2 * CW] + out1[:CW], 0.0)
-    ls_ref[...] = out0[2 * CW :] + out1[CW:]
+    out_ref[:CW] = jnp.where(row_in >= col_in, out0[:CW], 0.0)
+    out_ref[CW : 2 * CW] = jnp.where(row_in - PW >= col_in, out0[CW : 2 * CW] + out1[:CW], 0.0)
+    out_ref[2 * CW :] = out0[2 * CW :] + out1[CW:]
 
     own_quarter = pl.ds(pl.multiple_of(r * Q, Q), Q)
 
     @pl.when(s == 0)
     def _():
         d_hi, d_lo = split(dinv[0, own_quarter, :])
-        ls_ref[...] = mm(r0, d_hi, d_lo, 1)
+        out_ref[2 * CW :] = mm(r0, d_hi, d_lo, 1)
 
     @pl.when(s == 1)
     def _():
         d_hi, d_lo = split(dinv[1, own_quarter, :])
-        ls_ref[...] = mm(t1, d_hi, d_lo, 1)
+        out_ref[2 * CW :] = mm(t1, d_hi, d_lo, 1)
 
     @pl.when(x != 0)
     def _():
@@ -425,14 +441,11 @@
     hbm = pl.BlockSpec(memory_space=pltpu.HBM)
     dma = pltpu.SemaphoreType.DMA
     tile = (2 * CW, Q)
-    panel_factor, landmark_solution = pl.pallas_call(
+    out = pl.pallas_call(
         kernel,
-        out_shape=(
-            jax.ShapeDtypeStruct((2 * CW, Q), F32),
-            jax.ShapeDtypeStruct((NLAND, Q), F32),
-        ),
+        out_shape=pltpu.VMEM((2 * CW + NLAND, Q), F32),
         in_specs=[hbm] * 7,
-        out_specs=(vmem, vmem),
+        out_specs=vmem,
         scratch_shapes=[
             pltpu.VMEM((1, NROW * NODEQ), jnp.int32),
             pltpu.SMEM((1,), jnp.int32),
@@ -474,7 +487,7 @@
         child_factor, child_map, child_len, class_ids.reshape(64, Q), class_kappa,
         landmarks.reshape(1, 256), diag_inverse,
     )
-    return panel_factor.reshape(2, CW, 1, Q), landmark_solution.reshape(NLAND, 1, Q)
+    return out[: 2 * CW].reshape(2, CW, 1, Q), out[2 * CW :].reshape(NLAND, 1, Q)
 
 
 def solution(mesh):

time: 68.5 us -> 62.9 us (0.918)
  Pallas kernels: 64.2 us -> 60.2 us
  local copies, waits for them, and re-layouts: 2.8 us -> 1.24 us
    pallas_call x1, Pallas kernels: 64.2 us -> 60.2 us  [on_device(): pl.pallas_call(kernel, out_shape=pltpu.VMEM((2 * CW + NLAND, Q), F32), in...]
    unnamed x2 -> x0, local copies, waits for them, and re-layouts: 2.8 us -> none
    slice x0 -> x2, local copies, waits for them, and re-layouts: none -> 1.24 us  [the longest x1 0.63 us: on_device(): out[:2 * CW].reshape(2, CW, 1, Q)]
where the time goes in v3:
time: 62.9 us; the launch traced here: 62.7 us
  Pallas kernels  60.2 us (96%)
  between operations  1.29 us (2%)
  local copies, waits for them, and re-layouts  1.24 us (2%)
    pallas_call x1, Pallas kernels, on_device(): pl.pallas_call(kernel, out_shape=pltpu.VMEM((2 * CW + NLAND, Q), F32), in...  60.2 us

profile of v3, /device:TPU:1, one launch (start us, length us, event | category | flops | bytes accessed | tf_op | source)
XLA Modules:
  0.0 62.7 jit_solution(16410733446956725970)
XLA Ops:
  1.3 60.2 %shard_map.86 = f32[160,128]{1,0:T(8,128)S(1)} custom-call(f32[1,256,512]{2,1,0:T(8,128)} %factor_hbm.1, s32[1,2048]{1,0:T(1,128)} %map_hbm.1, s32[1]{0:T(128)S(6)} %copy.11.len_hbm, s32[64,128]{1,0:T(8,128)} %bitcast.9, f32[8]{0:T(128)} %kappa_hbm.1, s32[1,256]{1,0:T(1,128)} %bitcast.11, f32[2,512,512]{2,1,0:T(8,128)} %dinv_hbm.1), custom_call_target="tpu_custom_call" | custom-call | tf_op jit(solution)/shard_map/pallas_call | solution.py:444
  61.5 0.6 slice.7
  62.1 0.6 %slice.6 = f32[128,128]{1,0:T(8,128)} slice(f32[160,128]{1,0:T(8,128)S(1)} %shard_map.86), slice={[0:128], [0:128]} | slice | bytes 131072 | tf_op jit(solution)/shard_map/slice | solution.py:490

commit v4 on v3

--- a/solution.py
+++ b/solution.py
@@ -11,10 +11,8 @@
 
 NSUB, NROW, NCOL = 16, 4, 8
 NEAR = 4
-ORDER = (1, 4, 5, 6, 7)
+ORDER = (1, 2, 3, 4, 5)
 PW, Q, CW, KCH, NODEQ, NLAND = 512, 128, 64, 256, 512, 32
-CHUNKS = 2
-CROWS = 2 * CW // CHUNKS
 
 
 def dg(a, b, ca, cb):
@@ -50,10 +48,10 @@
     out_ref,
     map_ref, len_ref, ids_ref, kappa_ref, land_ref, factor, dinv, live_hi, live_lo, red_out, red_in, redl, pst,
     top_out, near_in, near_sum, far_in, near_all, top_all, front_top, rland, s_hi, s_lo,
-    first, ring_p, ring_m, fx,
+    terms, pre_p, pre_m, go_p, go_m, fx,
     ld_sem, red_s, red_r, redl_s, redl_r, near_s, near_r, far_s, far_r, all_s, all_r,
-    fy_s, fy_r, fx_s, fx_r, fwd_s, fwd_r, rl_s, rl_r,
-    rp_s, rp_r, rm_s, rm_r, xa_s, xa_r, xf_s, xf_r,
+    fy_s, fy_r, fc_s, fc_r, fx_s, fx_r, fwd_s, fwd_r, rl_s, rl_r,
+    pp_s, pp_r, pm_s, pm_r, gp_s, gp_r, gm_s, gm_r, xa_s, xa_r, xf_s, xf_r,
 ):
     s = lax.axis_index("sub")
     r = lax.axis_index("row")
@@ -64,6 +62,8 @@
     group = 2 * mod(r + x, NROW) + h
     right = {"sub": mod(s + 1, NSUB)}
     left = {"sub": mod(s + NSUB - 1, NSUB)}
+    right2 = {"sub": mod(s + 2, NSUB)}
+    left2 = {"sub": mod(s + NSUB - 2, NSUB)}
 
     def near_id(k):
         return {"sub": far * NEAR + mod(near + k, NEAR)}
@@ -84,7 +84,7 @@
 
     three = pl.ds(0, 3)
     of_redl, of_near, of_far = redl.at[three], near_in.at[three], far_in.at[three]
-    of_all, of_row, of_rland = top_all.at[pl.ds(0, 3 * 2 * CW // NEAR)], front_top.at[0, 0, three], rland.at[three]
+    of_all, of_row, of_rland = top_all.at[pl.ds(0, 3 * 2 * CW // NEAR)], front_top.at[0, 0, 0, three], rland.at[three]
 
     def arrived(bytes_of, sem):
         remote(bytes_of, bytes_of, sem, sem, other).wait_recv()
@@ -106,7 +106,7 @@
     load_dinv.start()
     barrier = pltpu.get_barrier_semaphore()
 
-    for peer in [right, left, other] + [make(k) for make in (near_id, far_id, row_id, x_id) for k in (1, 2, 3)]:
+    for peer in [right, left, right2, left2, other] + [make(k) for make in (near_id, far_id, row_id, x_id) for k in (1, 2, 3)]:
         pl.semaphore_signal(barrier, inc=1, device_id=peer, device_id_type=MESH)
 
     for copy in small:
@@ -131,7 +131,7 @@
     red_out[...] = reduced[: 2 * CW]
     redl[r] = reduced[2 * CW :]
 
-    pl.semaphore_wait(barrier, 15)
+    pl.semaphore_wait(barrier, 17)
 
     red_copy = remote(red_out, red_in, red_s.at[0], red_r.at[0], {"row": mod(r - x + NROW, NROW)})
 
@@ -200,6 +200,38 @@
     part_hi, part_lo = split(part)
     pst[...] = jnp.concatenate([part_hi[: 2 * CW], part_lo[: 2 * CW]], axis=0)
 
+    def term(k):
+        block_a, block_b = mod(s + 8 - k, NSUB), mod(s + 9 + k, NSUB)
+        place = rows_of((2 * Q, 1))
+        place = jnp.where(place < Q, block_a * Q + place, block_b * Q + place - Q)
+        place = jnp.where(target == place, 1.0, 0.0).astype(BF16)
+        both = dg(pst[...], place, 1, 1)
+        both = both[: 2 * CW] + both[2 * CW :]
+        terms[k, 0] = both[:, :Q]
+        terms[k, 1] = both[:, Q:]
+
+    pair_p = [remote(terms.at[2 * k, 0], pre_p.at[k], pp_s.at[k], pp_r.at[k], right) for k in range(4)]
+    pair_m = [remote(terms.at[2 * k + 1, 1], pre_m.at[k], pm_s.at[k], pm_r.at[k], left) for k in range(3)]
+    sum_p = [remote(pre_p.at[k], go_p.at[k], gp_s.at[k], gp_r.at[k], right2 if k < 3 else right) for k in range(4)]
+    sum_m = [remote(terms.at[0, 1], go_m.at[0], gm_s.at[0], gm_r.at[0], left2)] + [
+        remote(pre_m.at[k - 1], go_m.at[k], gm_s.at[k], gm_r.at[k], left2 if k < 3 else left) for k in (1, 2, 3)
+    ]
+
+    def pass_p(k):
+        pair_p[k].wait_recv()
+        if k == 0:
+            pre_p[k] += terms[1, 0]
+        else:
+            sum_p[k - 1].wait_recv()
+            pre_p[k] += go_p[k - 1] + terms[2 * k + 1, 0]
+        sum_p[k].start()
+
+    def pass_m(k):
+        pair_m[k - 1].wait_recv()
+        sum_m[k - 1].wait_recv()
+        pre_m[k - 1] += go_m[k - 1] + terms[2 * k, 1]
+        sum_m[k].start()
+
     place_top = jnp.where(target == rows_of((2 * Q, 1)), 1.0, 0.0).astype(BF16)
     top = dg(jnp.concatenate([part_hi, part_lo], axis=0), place_top, 1, 1)
     top = top[: 2 * CW + NLAND] + top[2 * CW + NLAND :]
@@ -220,62 +252,37 @@
         copy.start()
     near_in[near] = top_out[quarter_rows(near), :]
 
-    def contribution(block_a, block_b):
-        place = rows_of((2 * Q, 1))
-        place = jnp.where(place < Q, block_a * Q + place, block_b * Q + place - Q)
-        place = jnp.where(target == place, 1.0, 0.0).astype(BF16)
-        both = dg(pst[...], place, 1, 1)
-        both = both[: 2 * CW] + both[2 * CW :]
-        return both[:, :Q], both[:, Q:]
-
-    def ring_copy(src, ring, send, recv, step, chunk, where):
-        part_of = pl.ds(chunk * CROWS, CROWS)
-        return pltpu.make_async_remote_copy(
-            src_ref=src.at[part_of], dst_ref=ring.at[step, part_of],
-            send_sem=send.at[step, chunk], recv_sem=recv.at[step, chunk],
-            device_id=where, device_id_type=MESH,
-        )
-
-    def copy_p(src, step, chunk):
-        return ring_copy(src, ring_p, rp_s, rp_r, step, chunk, right)
-
-    def copy_m(src, step, chunk):
-        return ring_copy(src, ring_m, rm_s, rm_r, step, chunk, left)
-
-    to_right, to_left = contribution(mod(s + 8, NSUB), mod(s + 9, NSUB))
-    first[0] = to_right
-    first[1] = to_left
-    for chunk in range(CHUNKS):
-        copy_p(first.at[0], 0, chunk).start()
-        copy_m(first.at[1], 0, chunk).start()
-
-    def ring_step(t, carry):
-        to_right, to_left = contribution(mod(s + 8 - t, NSUB), mod(s + 9 + t, NSUB))
-        for chunk in range(CHUNKS):
-            part_of = pl.ds(chunk * CROWS, CROWS)
-            static = slice(chunk * CROWS, (chunk + 1) * CROWS)
-            copy_p(ring_p.at[t - 1], t - 1, chunk).wait_recv()
-            ring_p[t - 1, part_of, :] += to_right[static]
-            copy_p(ring_p.at[t - 1], t, chunk).start()
-            copy_m(ring_m.at[t - 1], t - 1, chunk).wait_recv()
-            ring_m[t - 1, part_of, :] += to_left[static]
-            copy_m(ring_m.at[t - 1], t, chunk).start()
-        return carry
+    term(0)
+    pair_p[0].start()
+    sum_m[0].start()
+    term(1)
+    pair_m[0].start()
+    term(2)
+    pair_p[1].start()
 
     far_copies = [remote(near_sum, far_in.at[far], far_s, far_r, far_id(k)) for k in (1, 2, 3)]
     all_copies = [remote(near_all, top_all.at[quarter_rows(near)], all_s, all_r, near_id(k)) for k in (1, 2, 3)]
-    row_copies = [remote(top_all.at[pl.ds(0, CW)], front_top.at[h, x, r], fy_s, fy_r, row_id(k)) for k in (1, 2, 3)]
+    half = CW // 2
+    row_copies = [
+        remote(top_all.at[pl.ds(0, half)], front_top.at[h, 0, x, r], fy_s, fy_r, row_id(k)) for k in (1, 2, 3)
+    ]
+    col_copies = [
+        remote(top_all.at[pl.ds(half, half)], front_top.at[h, 1, r, x], fc_s, fc_r, x_id(k)) for k in (1, 2, 3)
+    ]
     rland_copies = [
         remote(top_all.at[pl.ds(CW, 2 * NLAND)], rland.at[r], rl_s, rl_r, row_id(k)) for k in (1, 2, 3)
     ]
 
-    def x_copy(src_x, dst_x, where):
-        return remote(front_top.at[h, src_x], front_top.at[h, src_x], fx_s.at[dst_x], fx_r.at[src_x], where)
-
-    def fwd_copy(src_x, core):
-        return remote(front_top.at[core, src_x], front_top.at[core, src_x], fwd_s.at[src_x], fwd_r.at[src_x], other)
-
-    x_copies = [x_copy(x, mod(x + k, 4), x_id(k)) for k in (1, 2, 3)]
+    def wide_copy(part, src, dst, where):
+        piece = front_top.at[h, part, src]
+        return remote(piece, piece, fx_s.at[part, dst], fx_r.at[part, src], where)
+
+    def fwd_copy(part, src, core):
+        piece = front_top.at[core, part, src]
+        return remote(piece, piece, fwd_s.at[part, src], fwd_r.at[part, src], other)
+
+    x_copies = [wide_copy(0, x, mod(x + k, 4), x_id(k)) for k in (1, 2, 3)]
+    y_copies = [wide_copy(1, r, mod(r + k, 4), row_id(k)) for k in (1, 2, 3)]
 
     def near_step():
         arrived(of_near, near_r)
@@ -293,47 +300,54 @@
 
     def all_step():
         arrived(of_all, all_r)
-        for copy in row_copies + rland_copies:
+        for copy in row_copies + col_copies + rland_copies:
             copy.start()
-        front_top[h, x, r] = top_all[:CW]
+        front_top[h, 0, x, r] = top_all[:half]
+        front_top[h, 1, r, x] = top_all[half:CW]
         rland[r] = top_all[CW:]
 
     def row_step():
         arrived(of_row, fy_r)
         for copy in x_copies:
             copy.start()
-        fwd_copy(x, h).start()
+        arrived(of_row, fc_r)
+        for copy in y_copies:
+            copy.start()
+        fwd_copy(0, x, h).start()
+        fwd_copy(1, r, h).start()
 
     def x_step():
         for k in (1, 3, 2):
-            from_x = mod(x + k, 4)
-            x_copy(from_x, x, other).wait_recv()
-            fwd_copy(from_x, h).start()
-
-    done = 1
-    for top_step, ring_done in zip((near_step, far_step, all_step, row_step, x_step), ORDER):
-        if min(ring_done, 6) >= done:
-            lax.fori_loop(done, min(ring_done, 6) + 1, ring_step, 0)
-            done = min(ring_done, 6) + 1
-        if ring_done < 7:
-            top_step()
-    if done < 7:
-        lax.fori_loop(done, 7, ring_step, 0)
-
-    to_right, own = contribution(mod(s + 1, NSUB), s)
-    for chunk in range(CHUNKS):
-        part_of = pl.ds(chunk * CROWS, CROWS)
-        static = slice(chunk * CROWS, (chunk + 1) * CROWS)
-        copy_p(ring_p.at[6], 6, chunk).wait_recv()
-        ring_p[6, part_of, :] += to_right[static]
-        copy_p(ring_p.at[6], 7, chunk).start()
-    own = own + own_band
-    for chunk in range(CHUNKS):
-        part_of = pl.ds(chunk * CROWS, CROWS)
-        static = slice(chunk * CROWS, (chunk + 1) * CROWS)
-        copy_m(ring_m.at[6], 6, chunk).wait_recv()
-        copy_p(ring_p.at[7], 7, chunk).wait_recv()
-        fx[group, part_of, :] = own[static] + ring_m[6, part_of, :] + ring_p[7, part_of, :]
+            from_x, from_row = mod(x + k, 4), mod(r + k, 4)
+            wide_copy(0, from_x, x, other).wait_recv()
+            fwd_copy(0, from_x, h).start()
+            wide_copy(1, from_row, r, other).wait_recv()
+            fwd_copy(1, from_row, h).start()
+
+    top_steps = (near_step, far_step, all_step, row_step, x_step)
+
+    def tops(step):
+        for top_step, place in zip(top_steps, ORDER):
+            if place == step:
+                top_step()
+
+    for step in range(4):
+        pass_p(step)
+        if step:
+            pass_m(step)
+        tops(step + 1)
+        if step < 2:
+            term(2 * step + 3)
+            pair_m[step + 1].start()
+            term(2 * step + 4)
+            pair_p[step + 2].start()
+        if step == 2:
+            term(7)
+
+    own = terms[7, 1] + own_band
+    sum_m[3].wait_recv()
+    sum_p[3].wait_recv()
+    fx[group] = own + go_m[3] + go_p[3]
 
     def slot(px, ph):
         return 2 * mod(r + px, NROW) + ph
@@ -349,17 +363,25 @@
         copy.start()
     xfwd_copy(x, h).start()
 
-    for top_step, ring_done in zip((near_step, far_step, all_step, row_step, x_step), ORDER):
-        if ring_done == 7:
-            top_step()
+    tops(5)
 
     for k in range(4):
-        fwd_copy(k, 1 - h).wait_recv()
+        fwd_copy(0, k, 1 - h).wait_recv()
+        fwd_copy(1, k, 1 - h).wait_recv()
     arrived(of_rland, rl_r)
     f_hi, f_lo = split(
         jnp.concatenate(
             [
-                jnp.concatenate([front_top[g % 2, (g // 2 - k) % 4, k] for g in range(NCOL)], axis=0)
+                jnp.concatenate(
+                    [
+                        piece
+                        for g in range(NCOL)
+                        for piece in (
+                            front_top[g % 2, 0, (g // 2 - k) % 4, k], front_top[g % 2, 1, k, (g // 2 - k) % 4]
+                        )
+                    ],
+                    axis=0,
+                )
                 for k in range(NROW)
             ],
             axis=1,
@@ -414,26 +436,18 @@
         red_copy.wait_send()
 
     for bytes_of, sem in (
-        (of_redl, redl_s), (of_near, near_s), (of_far, far_s), (of_all, all_s), (of_row, fy_s), (of_rland, rl_s)
+        (of_redl, redl_s), (of_near, near_s), (of_far, far_s), (of_all, all_s), (of_row, fy_s), (of_row, fc_s), (of_rland, rl_s)
     ):
         departed(bytes_of, sem)
-    for copy in x_copies + xag_copies:
+    for copy in x_copies + y_copies + xag_copies:
         copy.wait_send()
     for k in range(4):
-        fwd_copy(k, h).wait_send()
+        fwd_copy(0, k, h).wait_send()
+        fwd_copy(1, k, h).wait_send()
     for k in range(4):
         xfwd_copy(k, h).wait_send()
-    for chunk in range(CHUNKS):
-        copy_p(first.at[0], 0, chunk).wait_send()
-        copy_m(first.at[1], 0, chunk).wait_send()
-
-        def sent_ring(t, carry):
-            copy_p(ring_p.at[t - 1], t, chunk).wait_send()
-            copy_m(ring_m.at[t - 1], t, chunk).wait_send()
-            return carry
-
-        lax.fori_loop(1, 7, sent_ring, 0)
-        copy_p(ring_p.at[6], 7, chunk).wait_send()
+    for copy in pair_p + pair_m + sum_p + sum_m:
+        copy.wait_send()
 
 
 def on_device(child_factor, child_map, child_len, class_ids, class_kappa, landmarks, diag_inverse):
@@ -466,18 +480,20 @@
             pltpu.VMEM((NEAR, 2 * CW // NEAR, Q), F32),
             pltpu.VMEM((2 * CW // NEAR, Q), F32),
             pltpu.VMEM(tile, F32),
-            pltpu.VMEM((2, 4, NROW, CW, Q), F32),
+            pltpu.VMEM((2, 2, 4, NROW, CW // 2, Q), F32),
             pltpu.VMEM((NROW, 2 * NLAND, Q), F32),
             pltpu.VMEM((2, PW, PW), BF16),
             pltpu.VMEM((2, PW, PW), BF16),
-            pltpu.VMEM((2,) + tile, F32),
-            pltpu.VMEM((8,) + tile, F32),
-            pltpu.VMEM((7,) + tile, F32),
+            pltpu.VMEM((8, 2) + tile, F32),
+            pltpu.VMEM((4,) + tile, F32),
+            pltpu.VMEM((3,) + tile, F32),
+            pltpu.VMEM((4,) + tile, F32),
+            pltpu.VMEM((4,) + tile, F32),
             pltpu.VMEM((NCOL,) + tile, F32),
             dma((7,)), dma((1,)), dma((1,)), dma, dma,
             dma, dma, dma, dma, dma, dma,
-            dma, dma, dma((4,)), dma((4,)), dma((4,)), dma((4,)), dma, dma,
-            dma((8, CHUNKS)), dma((8, CHUNKS)), dma((8, CHUNKS)), dma((8, CHUNKS)),
+            dma, dma, dma, dma, dma((2, 4)), dma((2, 4)), dma((2, 4)), dma((2, 4)), dma, dma,
+            dma((4,)), dma((4,)), dma((3,)), dma((3,)), dma((4,)), dma((4,)), dma((4,)), dma((4,)),
             dma((4,)), dma((4,)), dma((4,)), dma((4,)),
         ],
         compiler_params=pltpu.CompilerParams(

time: 62.9 us -> 60.7 us (0.965)
  Pallas kernels: 60.2 us -> 58 us
    pallas_call x1, Pallas kernels: 60.2 us -> 58 us  [on_device(): pl.pallas_call(kernel, out_shape=pltpu.VMEM((2 * CW + NLAND, Q), F32), in...]
where the time goes in v4:
time: 60.7 us; the launch traced here: 60.5 us
  Pallas kernels  58 us (96%)
  between operations  1.29 us (2%)
  local copies, waits for them, and re-layouts  1.24 us (2%)
    pallas_call x1, Pallas kernels, on_device(): pl.pallas_call(kernel, out_shape=pltpu.VMEM((2 * CW + NLAND, Q), F32), in...  58 us

profile of v4, /device:TPU:1, one launch (start us, length us, event | category | flops | bytes accessed | tf_op | source)
XLA Modules:
  0.0 60.5 jit_solution(6337187993999289521)
XLA Ops:
  1.3 58.0 %shard_map.86 = f32[160,128]{1,0:T(8,128)S(1)} custom-call(f32[1,256,512]{2,1,0:T(8,128)} %factor_hbm.1, s32[1,2048]{1,0:T(1,128)} %map_hbm.1, s32[1]{0:T(128)S(6)} %copy.11.len_hbm, s32[64,128]{1,0:T(8,128)} %bitcast.9, f32[8]{0:T(128)} %kappa_hbm.1, s32[1,256]{1,0:T(1,128)} %bitcast.11, f32[2,512,512]{2,1,0:T(8,128)} %dinv_hbm.1), custom_call_target="tpu_custom_call" | custom-call | tf_op jit(solution)/shard_map/pallas_call | solution.py:458
  59.3 0.6 %slice.7 = f32[32,128]{1,0:T(8,128)} slice(f32[160,128]{1,0:T(8,128)S(1)} %shard_map.86), slice={[128:160], [0:128]} | slice | bytes 32768 | tf_op jit(solution)/shard_map/slice | solution.py:506
  59.9 0.6 %slice.6 = f32[128,128]{1,0:T(8,128)} slice(f32[160,128]{1,0:T(8,128)S(1)} %shard_map.86), slice={[0:128], [0:128]} | slice | bytes 131072 | tf_op jit(solution)/shard_map/slice | solution.py:506

commit v5 on v4

--- a/solution.py
+++ b/solution.py
@@ -332,9 +332,9 @@
                 top_step()
 
     for step in range(4):
-        pass_p(step)
         if step:
             pass_m(step)
+        pass_p(step)
         tops(step + 1)
         if step < 2:
             term(2 * step + 3)

time: 60.7 us -> 60.1 us (level)
  no operation moved by 1% of the time
where the time goes in v5:
time: 60.1 us; the launch traced here: 60 us
  Pallas kernels  57.4 us (96%)
  between operations  1.29 us (2%)
  local copies, waits for them, and re-layouts  1.24 us (2%)
    pallas_call x1, Pallas kernels, on_device(): pl.pallas_call(kernel, out_shape=pltpu.VMEM((2 * CW + NLAND, Q), F32), in...  57.4 us

profile of v5, /device:TPU:1, one launch (start us, length us, event | category | flops | bytes accessed | tf_op | source)
XLA Modules:
  0.0 60.0 jit_solution(3190143997844792500)
XLA Ops:
  1.3 57.4 %shard_map.86 = f32[160,128]{1,0:T(8,128)S(1)} custom-call(f32[1,256,512]{2,1,0:T(8,128)} %factor_hbm.1, s32[1,2048]{1,0:T(1,128)} %map_hbm.1, s32[1]{0:T(128)S(6)} %copy.11.len_hbm, s32[64,128]{1,0:T(8,128)} %bitcast.9, f32[8]{0:T(128)} %kappa_hbm.1, s32[1,256]{1,0:T(1,128)} %bitcast.11, f32[2,512,512]{2,1,0:T(8,128)} %dinv_hbm.1), custom_call_target="tpu_custom_call" | custom-call | tf_op jit(solution)/shard_map/pallas_call | solution.py:458
  58.7 0.6 %slice.7 = f32[32,128]{1,0:T(8,128)} slice(f32[160,128]{1,0:T(8,128)S(1)} %shard_map.86), slice={[128:160], [0:128]} | slice | bytes 32768 | tf_op jit(solution)/shard_map/slice | solution.py:506
  59.3 0.6 %slice.6 = f32[128,128]{1,0:T(8,128)} slice(f32[160,128]{1,0:T(8,128)S(1)} %shard_map.86), slice={[0:128], [0:128]} | slice | bytes 131072 | tf_op jit(solution)/shard_map/slice | solution.py:506
